TPU v7x, 512 devices: a whole 4x8x8 slice. The times are simulated.
512 devices in a mesh: mode: 64 (over x, y, core), rank: 8 (over z).
Axes of the slice: x: 4, y: 8, z: 8, core: 2. Of those that a mesh axis runs over, the one named last changes fastest.
Arguments:
- start_core: float32 [1024, 128, 128], P('mode', 'rank'), may hold values from -108 to 108
- right_side: float32 [1024, 128, 128], P('mode', 'rank'), may hold values from -108 to 108
- left_interface: float32 [3, 128, 128], replicated, may hold values from -1 to 2
- right_interface: float32 [3, 128, 128], replicated, may hold values from -1 to 2
- couplings: float32 [3, 3, 3, 1024], P(None, None, None, 'mode'), may hold values from -5 to 5
Outputs:
- orthonormal_core: float32 [1024, 128, 128], P('mode', 'rank')
- triangle: float32 [128, 128], replicated
- next_interface: float32 [3, 128, 128], P(None, 'rank')
All inputs are finite; a program needn't handle non-finite values.
Results may differ from a plain program's by a relative error of at most 0.00027.
Values sent between devices are 32-bit elements; how exact they have to be, the bound alone decides.
No kernel may reach another device: no remote copies, remote signals or barrier semaphores. Data moves between devices by JAX's collectives and lax.ppermute only.
A program may use at most 64 MiB of HBM per device.

v0:
```python
import jax
import jax.numpy as jnp
from jax import lax
from jax.experimental import pallas as pl
from jax.experimental.pallas import tpu as pltpu
from jax.sharding import PartitionSpec as P

highest = lax.Precision.HIGHEST
W = 128
HALF = W // 2


def exchange(blocks, axis):
    return lax.all_to_all(blocks, axis, 0, 0, tiled=True)


def product(left, right):
    return jnp.dot(left, right, precision=highest, preferred_element_type=jnp.float32)


def product_t(left, right):
    return lax.dot_general(
        left,
        right,
        (((1,), (1,)), ((), ())),
        precision=highest,
        preferred_element_type=jnp.float32,
    )


def iotas(shape):
    return lax.broadcasted_iota(jnp.int32, shape, 0), lax.broadcasted_iota(jnp.int32, shape, 1)


def local_kernel(
    mine, low, high, table, left_ref, right_ref, blocks, owned, terms, mixed, coupled, moved, pair
):
    def slot(index):
        return mine[:, index].reshape(W, W)

    fields = [low[0:W], low[W : 2 * W], slot(0), slot(1), high[0:W], high[W : 2 * W]]
    sources = [low[2 * W : 3 * W], slot(2), slot(3), high[2 * W : 3 * W]]
    weights = [(low, 3 * W), (table, 0), (table, 32), (high, 3 * W)]
    right_rows = right_ref[...].reshape(3 * W, W)
    left_rows = left_ref[...].reshape(3 * W, W)
    left_lanes = jnp.concatenate([left_ref[0], left_ref[1], left_ref[2]], axis=1)

    def contract(values):
        for k in range(0, len(values), 2):
            both = product(right_rows, jnp.concatenate(values[k : k + 2], axis=1))
            terms[k] = both[:, :W]
            terms[k + 1] = both[:, W:]

    def rows_of(place):
        ref, base = place
        return [jnp.broadcast_to(ref[base + t : base + t + 1, :], (8, W)) for t in range(27)]

    def couple(place, first):
        cs = rows_of(place)

        def step(chunk, carry):
            at = pl.multiple_of(chunk * 8, 8)
            sums = [None] * 3
            for offset in range(3):
                for beta in range(3):
                    value = terms[first + offset, pl.ds(beta * W + at, 8), :]
                    for alpha in range(3):
                        part = cs[alpha * 9 + beta * 3 + offset] * value
                        sums[alpha] = part if sums[alpha] is None else sums[alpha] + part
            for alpha in range(3):
                coupled[pl.ds(at, 8), alpha * W : (alpha + 1) * W] = sums[alpha]
            return carry

        lax.fori_loop(0, W // 8, step, 0, unroll=2)
        return product_t(coupled[...], left_lanes)

    contract(fields)
    residual = [sources[i] - couple(weights[i], i) for i in range(4)]
    for i in range(4):
        pair[i] = fields[i + 1]
        pair[4 + i] = residual[i]
    owned[0:W] = residual[1]
    owned[W : 2 * W] = residual[2]
    contract(residual)
    along = jnp.zeros((1, 1), jnp.float32)
    energy = jnp.zeros((1, 1), jnp.float32)
    for i in range(2):
        image = couple(weights[1 + i], i)
        along = along + jnp.sum(pair[5 + i] * image, keepdims=True)
        energy = energy + jnp.sum(image * image, keepdims=True)

    for u in range(2):
        stack = pair[4 * u : 4 * u + 4].reshape(4 * W, W)
        mixed[4 * u : 4 * u + 4] = product_t(stack, left_rows).reshape(4, W, 3 * W)
    for i in range(2):
        cs = rows_of(weights[1 + i])

        def step(chunk, carry):
            u = chunk // (W // 8)
            at = pl.multiple_of((chunk % (W // 8)) * 8, 8)
            sums = [None] * 3
            for offset in range(3):
                for alpha in range(3):
                    value = mixed[4 * u + i + offset, pl.ds(at, 8), alpha * W : (alpha + 1) * W]
                    for beta in range(3):
                        part = cs[alpha * 9 + beta * 3 + offset] * value
                        sums[beta] = part if sums[beta] is None else sums[beta] + part
            for beta in range(3):
                moved[u, pl.ds(beta * W + at, 8), i * W : (i + 1) * W] = sums[beta]
            return carry

        lax.fori_loop(0, 2 * (W // 8), step, 0, unroll=2)

    both = jnp.concatenate(
        [
            jnp.concatenate([pair[1], pair[2]], axis=1),
            jnp.concatenate([pair[5], pair[6]], axis=1),
        ],
        axis=0,
    )
    forms = [product_t(moved[u], both) for u in range(2)]
    tables = [forms[0][:, :W], forms[0][:, W:] + forms[1][:, :W], forms[1][:, W:]]
    square = product_t(both, both)
    grams = [square[:W, :W], square[:W, W:] + square[W:, :W], square[W:, W:]]
    row, lane = iotas((HALF, W))
    for version in range(3):
        gram = grams[version]
        upper, under = gram[:HALF], gram[HALF:]
        for part in range(6):
            blocks[pl.ds(8 * version + part, HALF, stride=24), :] = tables[version][
                part * HALF : (part + 1) * HALF
            ]
        fold = jnp.where(lane <= row + HALF, under, pltpu.roll(upper, HALF, 1))
        blocks[pl.ds(8 * version + 6, HALF, stride=24), :] = fold
        diagonal = jnp.sum(jnp.where(lane == row, upper, 0.0), axis=1, keepdims=True)
        extra = jnp.where(lane == 0, diagonal, 0.0)
        if version == 0:
            extra = jnp.where(lane == 1, along, jnp.where(lane == 2, energy, extra))
        blocks[pl.ds(8 * version + 7, HALF, stride=24), :] = extra


def local_part(mine, low, high, table, left_interface, right_interface):
    vmem = pl.BlockSpec(memory_space=pltpu.VMEM)
    return pl.pallas_call(
        local_kernel,
        out_shape=(
            jax.ShapeDtypeStruct((HALF * 24, W), jnp.float32),
            jax.ShapeDtypeStruct((2 * W, W), jnp.float32),
        ),
        in_specs=[vmem] * 6,
        out_specs=(vmem, vmem),
        scratch_shapes=[
            pltpu.VMEM((6, 3 * W, W), jnp.float32),
            pltpu.VMEM((8, W, 3 * W), jnp.float32),
            pltpu.VMEM((W, 3 * W), jnp.float32),
            pltpu.VMEM((2, 3 * W, 2 * W), jnp.float32),
            pltpu.VMEM((8, W, W), jnp.float32),
        ],
        name="local_part",
    )(mine, low, high, table, left_interface, right_interface)


def combine_kernel(got, out, alpha_ref, *, ranks, scale):
    parts = []
    for version in range(3):
        total = got[8 * version : 8 * version + 8]
        for source in range(1, ranks):
            total = total + got[24 * source + 8 * version : 24 * source + 8 * version + 8]
        parts.append(total)
    row, lane = iotas((8, W))
    along = jnp.sum(jnp.where((row == 7) & (lane == 1), parts[0], 0.0), keepdims=True)
    energy = jnp.sum(jnp.where((row == 7) & (lane == 2), parts[0], 0.0), keepdims=True)
    alpha = jnp.broadcast_to(along, (8, W)) / jnp.broadcast_to(energy, (8, W))
    alpha_ref[...] = alpha
    block = (parts[0] + alpha * (parts[1] + alpha * parts[2])) * scale
    for m in range(HALF):
        out[8 * m : 8 * m + 8] = block


def combine_part(got, ranks, scale):
    vmem = pl.BlockSpec(memory_space=pltpu.VMEM)

    def kernel(*refs):
        combine_kernel(*refs, ranks=ranks, scale=scale)

    return pl.pallas_call(
        kernel,
        out_shape=(
            jax.ShapeDtypeStruct((HALF * 8, W), jnp.float32),
            jax.ShapeDtypeStruct((8, W), jnp.float32),
        ),
        in_specs=[vmem],
        out_specs=(vmem, vmem),
        name="combine_part",
    )(got)


def unfold(whole):
    table = jnp.concatenate([whole[:, part] for part in range(6)]).reshape(3, W, W)
    fold, extra = whole[:, 6], whole[:, 7]
    row, lane = iotas((HALF, W))
    under = jnp.where(lane <= row + HALF, fold, 0.0)
    upper = jnp.where((lane > row) & (lane < HALF), jnp.roll(fold, HALF, 1), 0.0)
    upper = upper + jnp.where(lane == row, extra[:, :1], 0.0)
    half = jnp.concatenate([jnp.zeros((HALF, W)), under]) + jnp.pad(upper, ((0, HALF), (0, 0))).T
    row, lane = iotas((W, W))
    return jnp.where(lane <= row, half, half.T), table


def shards(start_core, right_side, left_interface, right_interface, couplings):
    height, piece, width = start_core.shape
    ranks = lax.axis_size("rank")
    slabs = lax.axis_size("mode")
    count = slabs * ranks
    own = height // ranks
    assert width == W and own == 2 and slabs == HALF
    rank_index = lax.axis_index("rank")
    scale = 1.0 / (height * slabs * width)

    start = start_core.reshape(ranks, own, piece, width)
    right = right_side.reshape(ranks, own, piece, width)
    mine = exchange(jnp.concatenate([start, right], axis=1), "rank")

    table = lax.dynamic_slice_in_dim(couplings.reshape(27, height), rank_index * own, own, 1)
    table = jnp.pad(table, ((0, 5), (0, 0))).T[:, :, None]
    table = jnp.broadcast_to(table, (own, 32, width)).reshape(own * 32, width)
    forward = [(i, i + 1) for i in range(count - 1)]
    backward = [(target, source) for source, target in forward]

    def parcel(source, column):
        parts = [mine[:, slot].reshape(width, width) for slot in (0, 1, source)]
        return jnp.concatenate(parts + [table[32 * column : 32 * column + 32]], axis=0)

    low = lax.ppermute(parcel(3, 1), ("mode", "rank"), forward)
    high = lax.ppermute(parcel(2, 0), ("mode", "rank"), backward)
    blocks, owned = local_part(mine, low, high, table, left_interface, right_interface)

    block = jnp.sum(exchange(blocks.reshape(slabs, 24, width), "mode"), axis=0)
    block = exchange(jnp.broadcast_to(block, (ranks, 24, width)), "rank")
    block, alpha = combine_part(block.reshape(ranks * 24, width), ranks, scale)
    whole = exchange(block.reshape(slabs, 8, width), "mode")

    gram, tables = unfold(whole)
    lower = jnp.linalg.cholesky(gram)
    inverse = jax.scipy.linalg.solve_triangular(
        lower, jnp.eye(width, dtype=jnp.float32), lower=True
    )
    field = mine[:, :2].transpose(1, 0, 2, 3).reshape(own, width, width)
    core = field + alpha[0, 0] * owned.reshape(own, width, width)
    basis = jnp.einsum("bc,ica->bia", inverse, core, precision=highest)
    basis = basis.reshape(ranks, piece, own, width).transpose(0, 2, 1, 3)
    output = exchange(basis, "rank").reshape(height, piece, width)
    inverse_rows = lax.dynamic_slice_in_dim(inverse, rank_index * piece, piece, 0)
    interface = jnp.einsum("qc,ycd->yqd", inverse_rows, tables, precision=highest)
    interface = jnp.einsum("yqd,pd->yqp", interface, inverse, precision=highest)
    return (output, lower.T, interface)


def solution(mesh):
    placed = (
        P("mode", "rank", None),
        P("mode", "rank", None),
        P(),
        P(),
        P(None, None, None, "mode"),
    )
    return jax.shard_map(
        shards,
        mesh=mesh,
        in_specs=placed,
        out_specs=(P("mode", "rank", None), P(), P(None, "rank", None)),
        check_vma=False,
    )
```

profile of v0, /device:TPU:1, one launch (start us, length us, event | category | flops | bytes accessed | tf_op | source)
XLA Modules:
  0.0 156.5 jit_solution(14721196862318179711)
XLA Ops:
  0.6 1.7 %pad_maximum_fusion = f32[8,4,16,128]{3,2,1,0:T(8,128)} fusion(f32[8,2,16,128]{3,2,1,0:T(8,128)} %bitcast.99, f32[8,2,16,128]{3,2,1,0:T(8,128)} %bitcast.100), kind=kLoop, calls=%fused_computation.2 | loop fusion | flops 65536 | bytes 524288 | tf_op jit(solution)/shard_map/concatenate | solution.py:222
  2.3 11.0 %all-to-all-start = ((f32[8,4,16,128]{3,2,1,0:T(8,128)}), f32[8,4,16,128]{3,2,1,0:T(8,128)S(1)}, u32[]{:S(2)}, u32[]{:S(2)}) async-start(f32[8,4,16,128]{3,2,1,0:T(8,128)} %pad_maximum_fusion), calls=%async_computation | async-start | bytes 524288 | tf_op jit(solution)/shard_map/all_to_all | solution.py:14
  13.6 10.2 %all-to-all-done.mine = f32[8,4,16,128]{3,2,1,0:T(8,128)S(1)} async-done(((f32[8,4,16,128]{3,2,1,0:T(8,128)}), f32[8,4,16,128]{3,2,1,0:T(8,128)S(1)}, u32[]{:S(2)}, u32[]{:S(2)}) %all-to-all-start) | async-done | bytes 262176 | tf_op jit(solution)/shard_map/all_to_all | solution.py:14
  23.8 0.7 copy-done
  24.7 1.9 %collective-permute-start = (f32[416,128]{1,0:T(8,128)S(1)}, f32[416,128]{1,0:T(8,128)S(1)}, u32[]{:S(2)}, u32[]{:S(2)}) collective-permute-start(f32[416,128]{1,0:T(8,128)S(1)} %get-tuple-element.41), channel_id=1, source_target_pairs={{0,1},{1,2},{2,3},{3,4},{4,5},{5,6},{6,7},{7,8},{8,9},{9,10},{10,1... | collective-permute-start | bytes 638984 | tf_op jit(solution)/shard_map/ppermute | solution.py:234
  26.6 4.9 %collective-permute-start.1 = (f32[416,128]{1,0:T(8,128)S(1)}, f32[416,128]{1,0:T(8,128)S(1)}, u32[]{:S(2)}, u32[]{:S(2)}) collective-permute-start(f32[416,128]{1,0:T(8,128)S(1)} %get-tuple-element.40), channel_id=1, source_target_pairs={{1,0},{2,1},{3,2},{4,3},{5,4},{6,5},{7,6},{8,7},{9,8},{10,9},{11,1... | collective-permute-start | bytes 638984 | tf_op jit(solution)/shard_map/ppermute | solution.py:235
  31.6 1.4 collective-permute-done.low
  33.1 1.2 collective-permute-done.1.high
  34.2 0.7 broadcast_in_dim.32.table
  34.9 12.0 %local_part.1 = (f32[1536,128]{1,0:T(8,128)}, f32[256,128]{1,0:T(8,128)}) custom-call(f32[8,4,16,128]{3,2,1,0:T(8,128)} %copy-done, f32[416,128]{1,0:T(8,128)} %copy-done.3, f32[416,128]{1,0:T(8,128)} %copy-done.4, f32[64,128]{1,0:T(8,128)} %broadcast_in_dim.32.table, f32[3,128,128]{2,1,0:T(8,128)} %left_ref.1, f32[3,128,128]{2,1,0:T(8,128)} %right_ref.1), custom_call_target="tpu_custom_call" | custom-call | tf_op jit(solution)/shard_map/local_part/pallas_call | solution.py:144
  46.9 38.1 %all_to_all.25 = f32[64,24,128]{2,1,0:T(8,128)S(1)} all-to-all(f32[64,24,128]{2,1,0:T(8,128)} %bitcast.79), channel_id=1, replica_groups=mesh['mode'=64,'rank'=8] {'mode'}, dimensions={0} | all-to-all | bytes 1572864 | tf_op jit(solution)/shard_map/all_to_all | solution.py:14
  85.1 0.6 broadcast_in_dim.33
  85.7 4.1 %all-to-all-start.2 = ((f32[8,24,128]{2,1,0:T(8,128)}), f32[8,24,128]{2,1,0:T(8,128)S(1)}, u32[]{:S(2)}, u32[]{:S(2)}) async-start(f32[8,24,128]{2,1,0:T(8,128)} %broadcast_in_dim.33), calls=%async_computation.2 | async-start | bytes 196608 | tf_op jit(solution)/shard_map/all_to_all | solution.py:14
  89.8 7.4 %all-to-all-done.2 = f32[8,24,128]{2,1,0:T(8,128)S(1)} async-done(((f32[8,24,128]{2,1,0:T(8,128)}), f32[8,24,128]{2,1,0:T(8,128)S(1)}, u32[]{:S(2)}, u32[]{:S(2)}) %all-to-all-start.2) | async-done | bytes 98336 | tf_op jit(solution)/shard_map/all_to_all | solution.py:14
  97.3 0.6 copy-done.2
  97.9 1.7 %combine_part.1 = (f32[512,128]{1,0:T(8,128)}, f32[8,128]{1,0:T(8,128)}) custom-call(f32[192,128]{1,0:T(8,128)} %bitcast.85), custom_call_target="tpu_custom_call" | custom-call | tf_op jit(solution)/shard_map/combine_part/pallas_call | solution.py:186
  99.6 7.9 %all-to-all-start.3 = ((f32[64,8,128]{2,1,0:T(8,128)}), f32[64,8,128]{2,1,0:T(8,128)S(1)}, u32[]{:S(2)}, u32[]{:S(2)}) async-start(f32[64,8,128]{2,1,0:T(8,128)} %bitcast.87), calls=%async_computation.3 | async-start | bytes 524288 | tf_op jit(solution)/shard_map/all_to_all | solution.py:14
  107.6 1.2 slice.101
  108.8 0.7 broadcast_multiply_fusion
  109.5 10.0 %all-to-all-done.3 = f32[64,8,128]{2,1,0:T(8,128)S(1)} async-done(((f32[64,8,128]{2,1,0:T(8,128)}), f32[64,8,128]{2,1,0:T(8,128)S(1)}, u32[]{:S(2)}, u32[]{:S(2)}) %all-to-all-start.3) | async-done | bytes 262176 | tf_op jit(solution)/shard_map/all_to_all | solution.py:14
  120.4 11.7 %cholesky.17 = f32[128,128]{1,0:T(8,128)S(1)} custom-call(f32[128,128]{1,0:T(8,128)S(1)} %fusion.8), custom_call_target="Cholesky" | custom-call | tf_op jit(solution)/shard_map/jit(cholesky)/cholesky | solution.py:244
  132.1 0.6 compare_reduce_fusion
  132.8 0.7 fusion.11
  133.4 9.8 %custom-call.7 = f32[1,128,128]{1,2,0:T(8,128)S(1)} custom-call(f32[1,128,128]{2,1,0:T(8,128)S(1)} %get-tuple-element.43), custom_call_target="InvertDiagBlocksLowerTriangular" | custom-call | tf_op jit(solution)/shard_map/jit(_solve_triangular)/triangular_solve | solution.py:245
  143.3 0.2 fusion.6
  143.5 0.9 convolution_bitcast_fusion
  144.4 3.4 %all-to-all-start.4 = ((f32[8,2,16,128]{3,2,1,0:T(8,128)}), f32[8,2,16,128]{3,2,1,0:T(8,128)S(1)}, u32[]{:S(2)}, u32[]{:S(2)}) async-start(f32[8,2,16,128]{3,2,1,0:T(8,128)} %convolution_bitcast_fusion), calls=%async_computation.4 | async-start | bytes 262144 | tf_op jit(solution)/shard_map/all_to_all | solution.py:14
  147.9 0.3 convolution_bitcast_fusion.1
  148.1 0.7 copy.58
  148.9 0.8 fusion.4
  149.7 6.2 %all-to-all-done.4 = f32[8,2,16,128]{3,2,1,0:T(8,128)S(1)} async-done(((f32[8,2,16,128]{3,2,1,0:T(8,128)}), f32[8,2,16,128]{3,2,1,0:T(8,128)S(1)}, u32[]{:S(2)}, u32[]{:S(2)}) %all-to-all-start.4) | async-done | bytes 131104 | tf_op jit(solution)/shard_map/all_to_all | solution.py:14
  155.9 0.7 copy.75
  (46 shorter events, 1.6 us)
Async XLA Ops:
  2.3 11.0 %copy-start.6 = (f32[3,3,3,16]{3,2,1,0:T(4,128)S(1)}, f32[3,3,3,16]{3,2,1,0:T(4,128)}, u32[]{:S(2)}) copy-start(f32[3,3,3,16]{3,2,1,0:T(4,128)} %param.9) | copy-start | bytes 5188
  2.3 21.5 %all-to-all-start = ((f32[8,4,16,128]{3,2,1,0:T(8,128)}), f32[8,4,16,128]{3,2,1,0:T(8,128)S(1)}, u32[]{:S(2)}, u32[]{:S(2)}) async-start(f32[8,4,16,128]{3,2,1,0:T(8,128)} %pad_maximum_fusion), calls=%async_computation | async-start | bytes 524288 | tf_op jit(solution)/shard_map/all_to_all | solution.py:14
  23.8 0.7 copy-start
  24.7 8.4 %collective-permute-start = (f32[416,128]{1,0:T(8,128)S(1)}, f32[416,128]{1,0:T(8,128)S(1)}, u32[]{:S(2)}, u32[]{:S(2)}) collective-permute-start(f32[416,128]{1,0:T(8,128)S(1)} %get-tuple-element.41), channel_id=1, source_target_pairs={{0,1},{1,2},{2,3},{3,4},{4,5},{5,6},{6,7},{7,8},{8,9},{9,10},{10,1... | collective-permute-start | bytes 638984 | tf_op jit(solution)/shard_map/ppermute | solution.py:234
  26.6 7.6 %collective-permute-start.1 = (f32[416,128]{1,0:T(8,128)S(1)}, f32[416,128]{1,0:T(8,128)S(1)}, u32[]{:S(2)}, u32[]{:S(2)}) collective-permute-start(f32[416,128]{1,0:T(8,128)S(1)} %get-tuple-element.40), channel_id=1, source_target_pairs={{1,0},{2,1},{3,2},{4,3},{5,4},{6,5},{7,6},{8,7},{9,8},{10,9},{11,1... | collective-permute-start | bytes 638984 | tf_op jit(solution)/shard_map/ppermute | solution.py:235
  33.1 1.9 %copy-start.3 = (f32[416,128]{1,0:T(8,128)}, f32[416,128]{1,0:T(8,128)S(1)}, u32[]{:S(2)}) copy-start(f32[416,128]{1,0:T(8,128)S(1)} %collective-permute-done.low) | copy-start | bytes 638980
  34.2 0.7 copy-start.4
  85.7 11.6 %all-to-all-start.2 = ((f32[8,24,128]{2,1,0:T(8,128)}), f32[8,24,128]{2,1,0:T(8,128)S(1)}, u32[]{:S(2)}, u32[]{:S(2)}) async-start(f32[8,24,128]{2,1,0:T(8,128)} %broadcast_in_dim.33), calls=%async_computation.2 | async-start | bytes 196608 | tf_op jit(solution)/shard_map/all_to_all | solution.py:14
  97.3 0.6 copy-start.2
  99.6 9.2 %copy-start.5 = (f32[256,128]{1,0:T(8,128)S(1)}, f32[256,128]{1,0:T(8,128)}, u32[]{:S(2)}) copy-start(f32[256,128]{1,0:T(8,128)} %get-tuple-element.10) | copy-start | bytes 393220
  99.6 19.9 %all-to-all-start.3 = ((f32[64,8,128]{2,1,0:T(8,128)}), f32[64,8,128]{2,1,0:T(8,128)S(1)}, u32[]{:S(2)}, u32[]{:S(2)}) async-start(f32[64,8,128]{2,1,0:T(8,128)} %bitcast.87), calls=%async_computation.3 | async-start | bytes 524288 | tf_op jit(solution)/shard_map/all_to_all | solution.py:14
  107.6 1.9 %copy-start.1 = (f32[8,4,16,128]{3,2,1,0:T(8,128)S(1)}, f32[8,4,16,128]{3,2,1,0:T(8,128)}, u32[]{:S(2)}) copy-start(f32[8,4,16,128]{3,2,1,0:T(8,128)} %copy-done) | copy-start | bytes 786436
  144.4 11.5 %all-to-all-start.4 = ((f32[8,2,16,128]{3,2,1,0:T(8,128)}), f32[8,2,16,128]{3,2,1,0:T(8,128)S(1)}, u32[]{:S(2)}, u32[]{:S(2)}) async-start(f32[8,2,16,128]{3,2,1,0:T(8,128)} %convolution_bitcast_fusion), calls=%async_computation.4 | async-start | bytes 262144 | tf_op jit(solution)/shard_map/all_to_all | solution.py:14
where the time goes:
time: 158 us; the launch traced here: 157 us
  blocking collectives  38.1 us (24%)
  waiting for transfers between devices  36.4 us (23%)
  starting transfers between devices  33.2 us (21%)
  other arithmetic  25.6 us (16%)
  Pallas kernels  13.7 us (9%)
  local copies, waits for them, and re-layouts  6.42 us (4%)
  matrix products  2.25 us (1%)
    all_to_all x1, blocking collectives, exchange(): return lax.all_to_all(blocks, axis, 0, 0, tiled=True)  38.1 us
    all_to_all x4, waiting for transfers between devices, exchange(): return lax.all_to_all(blocks, axis, 0, 0, tiled=True)  33.8 us
    all_to_all x4, starting transfers between devices, exchange(): return lax.all_to_all(blocks, axis, 0, 0, tiled=True)  26.4 us
    another operation x3, other arithmetic, shards(): lower = jnp.linalg.cholesky(gram)  12.4 us
    pallas_call x1, Pallas kernels, local_part(): pl.pallas_call(local_kernel, out_shape=(jax.ShapeDtypeStruct((HALF * 24,...  12 us
    another operation x1, other arithmetic, shards(): jax.scipy.linalg.solve_triangular(lower, jnp.eye(width, dtype=jnp.float32...  9.81 us
    ppermute x1, starting transfers between devices, shards(): high = lax.ppermute(parcel(2, 0), ('mode', 'rank'), backward)  4.85 us
  transfers between devices with their start and end apart: 6, of which 6 were waited for; matrix products, arithmetic and copies ran while one was open for 3% of the time, Pallas kernels for 0%

commit v1 on v0

--- a/solution.py
+++ b/solution.py
@@ -3,11 +3,13 @@
 from jax import lax
 from jax.experimental import pallas as pl
 from jax.experimental.pallas import tpu as pltpu
+from jax.sharding import Mesh
 from jax.sharding import PartitionSpec as P
 
 highest = lax.Precision.HIGHEST
 W = 128
 HALF = W // 2
+SIZE = 16
 
 
 def exchange(blocks, axis):
@@ -173,7 +175,7 @@
     alpha = jnp.broadcast_to(along, (8, W)) / jnp.broadcast_to(energy, (8, W))
     alpha_ref[...] = alpha
     block = (parts[0] + alpha * (parts[1] + alpha * parts[2])) * scale
-    for m in range(HALF):
+    for m in range(8):
         out[8 * m : 8 * m + 8] = block
 
 
@@ -186,7 +188,7 @@
     return pl.pallas_call(
         kernel,
         out_shape=(
-            jax.ShapeDtypeStruct((HALF * 8, W), jnp.float32),
+            jax.ShapeDtypeStruct((8 * 8, W), jnp.float32),
             jax.ShapeDtypeStruct((8, W), jnp.float32),
         ),
         in_specs=[vmem],
@@ -195,22 +197,108 @@
     )(got)
 
 
-def unfold(whole):
-    table = jnp.concatenate([whole[:, part] for part in range(6)]).reshape(3, W, W)
-    fold, extra = whole[:, 6], whole[:, 7]
+def factor_kernel(whole, alpha_ref, mine, owned, basis, triangle, inverse, table):
     row, lane = iotas((HALF, W))
+    fold = whole[pl.ds(6, HALF, stride=8), :]
+    extra = whole[pl.ds(7, HALF, stride=8), :]
     under = jnp.where(lane <= row + HALF, fold, 0.0)
-    upper = jnp.where((lane > row) & (lane < HALF), jnp.roll(fold, HALF, 1), 0.0)
-    upper = upper + jnp.where(lane == row, extra[:, :1], 0.0)
-    half = jnp.concatenate([jnp.zeros((HALF, W)), under]) + jnp.pad(upper, ((0, HALF), (0, 0))).T
+    upper = jnp.where((lane > row) & (lane < HALF), pltpu.roll(fold, HALF, 1), 0.0)
+    upper = upper + jnp.where(lane == row, jnp.broadcast_to(extra[:, :1], (HALF, W)), 0.0)
+    zero = jnp.zeros((HALF, W), jnp.float32)
+    lower_part = jnp.concatenate([zero, under], axis=0)
+    upper_part = jnp.concatenate([upper, zero], axis=0)
     row, lane = iotas((W, W))
-    return jnp.where(lane <= row, half, half.T), table
+    lower_part = lower_part + jnp.where(lane < row, upper_part.T, 0.0)
+    table[:, :W] = lower_part.T + jnp.where(lane < row, lower_part, 0.0) + upper_part - jnp.where(
+        lane > row, upper_part, 0.0
+    )
+    table[:, W:] = jnp.where(lane == row, 1.0, 0.0)
+
+    sub, across = iotas((SIZE, W))
+    for first in range(0, W, SIZE):
+        last = first + SIZE
+        panel = table[first:last, :]
+        left, right = panel[:, :W], panel[:, W:]
+        columns = [
+            jnp.broadcast_to(left[:, first + k : first + k + 1], (SIZE, W)) for k in range(SIZE)
+        ]
+        for k in range(SIZE):
+            pivot = jnp.broadcast_to(columns[k][k : k + 1, :], (SIZE, W))
+            root = lax.rsqrt(pivot)
+            root = root * (1.5 - 0.5 * pivot * (root * root))
+            factor = columns[k] * root
+
+            def eliminate(value):
+                scaled = jnp.broadcast_to(value[k : k + 1, :], (SIZE, W)) * root
+                return jnp.where(sub == k, scaled, jnp.where(sub > k, value - factor * scaled, value))
+
+            left, right = eliminate(left), eliminate(right)
+            for j in range(k + 1, SIZE):
+                columns[j] = eliminate(columns[j])
+        left = jnp.where(across >= sub + first, left, 0.0)
+        triangle[first:last, :] = left
+        inverse[first:last, :] = right
+        if last < W:
+            done = jnp.concatenate([left, right], axis=1)
+            change = lax.dot_general(
+                left,
+                done,
+                (((0,), (0,)), ((), ())),
+                precision=highest,
+                preferred_element_type=jnp.float32,
+            )
+            table[last:, :] = table[last:, :] - change[last:, :]
+
+    alpha = alpha_ref[0:1, :]
+    core = [
+        mine[:, i].reshape(W, W) + alpha * owned[i * W : (i + 1) * W] for i in range(2)
+    ]
+    both = product(inverse[...], jnp.concatenate(core, axis=1))
+    for i in range(2):
+        basis[:, i] = both[:, i * W : (i + 1) * W].reshape(basis.shape[0], basis.shape[2], W)
+
+
+def interface_kernel(rank, whole, inverse, out):
+    rows = out.shape[1]
+    start = pl.multiple_of(rank[0] * rows, rows)
+    mine = inverse[pl.ds(start, rows), :]
+    parts = []
+    for beta in range(3):
+        halves = [whole[pl.ds(2 * beta + h, HALF, stride=8), :] for h in range(2)]
+        parts.append(product(mine, jnp.concatenate(halves, axis=0)))
+    result = product_t(jnp.concatenate(parts, axis=0), inverse[...])
+    out[...] = result.reshape(3, rows, W)
+
+
+def final_part(whole, alpha, mine, owned, rank):
+    vmem = pl.BlockSpec(memory_space=pltpu.VMEM)
+    ranks, _, piece, _ = mine.shape
+    basis, triangle, inverse = pl.pallas_call(
+        factor_kernel,
+        out_shape=(
+            jax.ShapeDtypeStruct((ranks, 2, piece, W), jnp.float32),
+            jax.ShapeDtypeStruct((W, W), jnp.float32),
+            jax.ShapeDtypeStruct((W, W), jnp.float32),
+        ),
+        in_specs=[vmem] * 4,
+        out_specs=(vmem,) * 3,
+        scratch_shapes=[pltpu.VMEM((W, 2 * W), jnp.float32)],
+        name="factor_part",
+    )(whole, alpha, mine, owned)
+    interface = pl.pallas_call(
+        interface_kernel,
+        out_shape=jax.ShapeDtypeStruct((3, piece, W), jnp.float32),
+        in_specs=[pl.BlockSpec(memory_space=pltpu.SMEM), vmem, vmem],
+        out_specs=vmem,
+        name="interface_part",
+    )(rank, whole, inverse)
+    return basis, triangle, interface
 
 
 def shards(start_core, right_side, left_interface, right_interface, couplings):
     height, piece, width = start_core.shape
     ranks = lax.axis_size("rank")
-    slabs = lax.axis_size("mode")
+    slabs = lax.axis_size(("x", "y", "core"))
     count = slabs * ranks
     own = height // ranks
     assert width == W and own == 2 and slabs == HALF
@@ -231,43 +319,31 @@
         parts = [mine[:, slot].reshape(width, width) for slot in (0, 1, source)]
         return jnp.concatenate(parts + [table[32 * column : 32 * column + 32]], axis=0)
 
-    low = lax.ppermute(parcel(3, 1), ("mode", "rank"), forward)
-    high = lax.ppermute(parcel(2, 0), ("mode", "rank"), backward)
+    low = lax.ppermute(parcel(3, 1), ("x", "y", "core", "rank"), forward)
+    high = lax.ppermute(parcel(2, 0), ("x", "y", "core", "rank"), backward)
     blocks, owned = local_part(mine, low, high, table, left_interface, right_interface)
 
-    block = jnp.sum(exchange(blocks.reshape(slabs, 24, width), "mode"), axis=0)
+    block = jnp.sum(exchange(blocks.reshape(8, 192, width), ("x", "core")), axis=0)
+    block = jnp.sum(exchange(block.reshape(8, 24, width), "y"), axis=0)
     block = exchange(jnp.broadcast_to(block, (ranks, 24, width)), "rank")
     block, alpha = combine_part(block.reshape(ranks * 24, width), ranks, scale)
-    whole = exchange(block.reshape(slabs, 8, width), "mode")
-
-    gram, tables = unfold(whole)
-    lower = jnp.linalg.cholesky(gram)
-    inverse = jax.scipy.linalg.solve_triangular(
-        lower, jnp.eye(width, dtype=jnp.float32), lower=True
-    )
-    field = mine[:, :2].transpose(1, 0, 2, 3).reshape(own, width, width)
-    core = field + alpha[0, 0] * owned.reshape(own, width, width)
-    basis = jnp.einsum("bc,ica->bia", inverse, core, precision=highest)
-    basis = basis.reshape(ranks, piece, own, width).transpose(0, 2, 1, 3)
+    block = exchange(block.reshape(8, 8, width), "y").reshape(64, width)
+    whole = exchange(jnp.broadcast_to(block, (8, 64, width)), ("x", "core"))
+
+    rank = jnp.full((1,), rank_index, jnp.int32)
+    basis, triangle, interface = final_part(whole.reshape(512, width), alpha, mine, owned, rank)
     output = exchange(basis, "rank").reshape(height, piece, width)
-    inverse_rows = lax.dynamic_slice_in_dim(inverse, rank_index * piece, piece, 0)
-    interface = jnp.einsum("qc,ycd->yqd", inverse_rows, tables, precision=highest)
-    interface = jnp.einsum("yqd,pd->yqp", interface, inverse, precision=highest)
-    return (output, lower.T, interface)
+    return (output, triangle, interface)
 
 
 def solution(mesh):
-    placed = (
-        P("mode", "rank", None),
-        P("mode", "rank", None),
-        P(),
-        P(),
-        P(None, None, None, "mode"),
-    )
+    names = ("x", "y", "core")
+    fine = Mesh(mesh.devices.reshape(4, 8, 2, 8), names + ("rank",))
+    placed = (P(names, "rank", None), P(names, "rank", None), P(), P(), P(None, None, None, names))
     return jax.shard_map(
         shards,
-        mesh=mesh,
+        mesh=fine,
         in_specs=placed,
-        out_specs=(P("mode", "rank", None), P(), P(None, "rank", None)),
+        out_specs=(P(names, "rank", None), P(), P(None, "rank", None)),
         check_vma=False,
     )

time: 158 us -> 140 us (0.89)
  blocking collectives: 38.1 us -> 69.7 us
  other arithmetic: 25.6 us -> 1.91 us
  waiting for transfers between devices: 36.4 us -> 20.9 us
  starting transfers between devices: 33.2 us -> 19.6 us
  Pallas kernels: 13.7 us -> 23.6 us
  local copies, waits for them, and re-layouts: 6.42 us -> 2.55 us
  matrix products: 2.25 us -> 0 us
    all_to_all x1 -> x5, blocking collectives: 38.1 us -> 69.7 us  [exchange(): return lax.all_to_all(blocks, axis, 0, 0, tiled=True)]
    another operation x4 -> x0, other arithmetic: 22.2 us -> none  [the longest x3 12.4 us: shards(): lower = jnp.linalg.cholesky(gram)]
    all_to_all x4 -> x2, waiting for transfers between devices: 33.8 us -> 15.7 us  [exchange(): return lax.all_to_all(blocks, axis, 0, 0, tiled=True)]
    all_to_all x4 -> x2, starting transfers between devices: 26.4 us -> 14.4 us  [exchange(): return lax.all_to_all(blocks, axis, 0, 0, tiled=True)]
    pallas_call x1 -> x3, Pallas kernels: 1.75 us -> 11.6 us  [the longest x1 7.82 us: final_part(): pl.pallas_call(factor_kernel, out_shape=(jax.ShapeDtypeStruct((ranks, 2,...]
    ppermute x2, waiting for transfers between devices: 2.6 us -> 5.23 us  [the longest x1 4.1 us: shards(): low = lax.ppermute(parcel(3, 1), ('x', 'y', 'core', 'rank'), forward)]
    dot_general x3 -> x0, matrix products: 2 us -> none  [the longest x1 0.92 us: shards(): basis = jnp.einsum('bc,ica->bia', inverse, core, precision=highest)]
  transfers between devices with their start and end apart: 6 -> 4, of which waited for: 6 -> 4; matrix products, arithmetic and copies ran while one was open for 3% -> 0% of each run, Pallas kernels for 0% -> 2%
where the time goes in v1:
time: 140 us; the launch traced here: 139 us
  blocking collectives  69.7 us (50%)
  Pallas kernels  23.6 us (17%)
  waiting for transfers between devices  20.9 us (15%)
  starting transfers between devices  19.6 us (14%)
  local copies, waits for them, and re-layouts  2.55 us (2%)
  other arithmetic  1.91 us (1%)
    all_to_all x5, blocking collectives, exchange(): return lax.all_to_all(blocks, axis, 0, 0, tiled=True)  69.7 us
    all_to_all x2, waiting for transfers between devices, exchange(): return lax.all_to_all(blocks, axis, 0, 0, tiled=True)  15.7 us
    all_to_all x2, starting transfers between devices, exchange(): return lax.all_to_all(blocks, axis, 0, 0, tiled=True)  14.4 us
    pallas_call x1, Pallas kernels, local_part(): pl.pallas_call(local_kernel, out_shape=(jax.ShapeDtypeStruct((HALF * 24,...  12 us
    pallas_call x1, Pallas kernels, final_part(): pl.pallas_call(factor_kernel, out_shape=(jax.ShapeDtypeStruct((ranks, 2,...  7.82 us
    ppermute x1, waiting for transfers between devices, shards(): low = lax.ppermute(parcel(3, 1), ('x', 'y', 'core', 'rank'), forward)  4.1 us
    ppermute x1, starting transfers between devices, shards(): low = lax.ppermute(parcel(3, 1), ('x', 'y', 'core', 'rank'), forward)  2.97 us
  transfers between devices with their start and end apart: 4, of which 4 were waited for; matrix products, arithmetic and copies ran while one was open for 0% of the time, Pallas kernels for 2%

profile of v1, /device:TPU:1, one launch (start us, length us, event | category | flops | bytes accessed | tf_op | source)
XLA Modules:
  0.0 139.0 jit_solution(10179399060917772225)
XLA Ops:
  0.6 1.7 %pad_maximum_fusion = f32[8,4,16,128]{3,2,1,0:T(8,128)} fusion(f32[8,2,16,128]{3,2,1,0:T(8,128)} %bitcast.27, f32[8,2,16,128]{3,2,1,0:T(8,128)} %bitcast.28), kind=kLoop, calls=%fused_computation | loop fusion | flops 65536 | bytes 524288 | tf_op jit(solution)/shard_map/concatenate | solution.py:310
  2.3 0.0 copy-start.3
  2.3 11.0 %all-to-all-start = ((f32[8,4,16,128]{3,2,1,0:T(8,128)}), f32[8,4,16,128]{3,2,1,0:T(8,128)S(1)}, u32[]{:S(2)}, u32[]{:S(2)}) async-start(f32[8,4,16,128]{3,2,1,0:T(8,128)} %pad_maximum_fusion), calls=%async_computation | async-start | bytes 524288 | tf_op jit(solution)/shard_map/all_to_all | solution.py:16
  13.3 0.0 copy-done.3
  13.3 0.1 constant_dynamic-slice_fusion
  13.4 0.2 slice_reduce_fusion
  13.6 10.2 %all-to-all-done.mine = f32[8,4,16,128]{3,2,1,0:T(8,128)S(1)} async-done(((f32[8,4,16,128]{3,2,1,0:T(8,128)}), f32[8,4,16,128]{3,2,1,0:T(8,128)S(1)}, u32[]{:S(2)}, u32[]{:S(2)}) %all-to-all-start) | async-done | bytes 262176 | tf_op jit(solution)/shard_map/all_to_all | solution.py:16
  23.8 0.0 copy-start
  23.8 0.7 copy-done
  24.5 0.2 fusion.1
  24.7 2.3 %collective-permute-start.1 = (f32[416,128]{1,0:T(8,128)S(1)}, f32[416,128]{1,0:T(8,128)S(1)}, u32[]{:S(2)}, u32[]{:S(2)}) collective-permute-start(f32[416,128]{1,0:T(8,128)S(1)} %get-tuple-element.23), channel_id=1, source_target_pairs={{1,0},{2,1},{3,2},{4,3},{5,4},{6,5},{7,6},{8,7},{9,8},{10,9},{11,1... | collective-permute-start | bytes 638984 | tf_op jit(solution)/shard_map/ppermute | solution.py:323
  27.0 3.0 %collective-permute-start = (f32[416,128]{1,0:T(8,128)S(1)}, f32[416,128]{1,0:T(8,128)S(1)}, u32[]{:S(2)}, u32[]{:S(2)}) collective-permute-start(f32[416,128]{1,0:T(8,128)S(1)} %get-tuple-element.24), channel_id=1, source_target_pairs={{0,1},{1,2},{2,3},{3,4},{4,5},{5,6},{6,7},{7,8},{8,9},{9,10},{10,1... | collective-permute-start | bytes 638984 | tf_op jit(solution)/shard_map/ppermute | solution.py:322
  30.0 0.1 copy.11
  30.1 0.1 broadcast_in_dim.17
  30.1 1.1 collective-permute-done.1.high
  31.3 0.0 copy-start.1
  31.3 4.1 %collective-permute-done.low = f32[416,128]{1,0:T(8,128)S(1)} collective-permute-done((f32[416,128]{1,0:T(8,128)S(1)}, f32[416,128]{1,0:T(8,128)S(1)}, u32[]{:S(2)}, u32[]{:S(2)}) %collective-permute-start) | collective-permute-done | bytes 213024 | tf_op jit(solution)/shard_map/ppermute | solution.py:322
  35.4 0.7 broadcast_in_dim.18.table
  36.1 0.0 copy-done.1
  36.1 0.0 copy-done.2
  36.1 12.0 %local_part.1 = (f32[1536,128]{1,0:T(8,128)}, f32[256,128]{1,0:T(8,128)}) custom-call(f32[8,4,16,128]{3,2,1,0:T(8,128)} %copy-done, f32[416,128]{1,0:T(8,128)} %copy-done.2, f32[416,128]{1,0:T(8,128)} %copy-done.1, f32[64,128]{1,0:T(8,128)} %broadcast_in_dim.18.table, f32[3,128,128]{2,1,0:T(8,128)} %left_ref.1, f32[3,128,128]{2,1,0:T(8,128)} %right_ref.1), custom_call_target="tpu_custom_call" | custom-call | tf_op jit(solution)/shard_map/local_part/pallas_call | solution.py:146
  48.1 21.4 %all_to_all.35 = f32[8,192,128]{2,1,0:T(8,128)S(1)} all-to-all(f32[8,192,128]{2,1,0:T(8,128)} %bitcast.18), channel_id=1, replica_groups=mesh['x'=4,'y'=8,'core'=2,'rank'=8] {'x','core'}, dimensions={0} | all-to-all | bytes 1572864 | tf_op jit(solution)/shard_map/all_to_all | solution.py:16
  69.5 13.3 %all_to_all.36 = f32[8,24,128]{2,1,0:T(8,128)S(1)} all-to-all(f32[8,24,128]{2,1,0:T(8,128)S(1)} %bitcast.21), channel_id=1, replica_groups=mesh['x'=4,'y'=8,'core'=2,'rank'=8] {'y'}, dimensions={0} | all-to-all | bytes 196608 | tf_op jit(solution)/shard_map/all_to_all | solution.py:16
  82.8 10.6 %all_to_all.37 = f32[8,24,128]{2,1,0:T(8,128)} all-to-all(f32[8,24,128]{2,1,0:T(8,128)S(1)} %broadcast_in_dim.19), channel_id=1, replica_groups=mesh['x'=4,'y'=8,'core'=2,'rank'=8] {'rank'}, dimensions={0} | all-to-all | bytes 196608 | tf_op jit(solution)/shard_map/all_to_all | solution.py:16
  93.4 1.6 %combine_part.1 = (f32[64,128]{1,0:T(8,128)}, f32[8,128]{1,0:T(8,128)}) custom-call(f32[192,128]{1,0:T(8,128)} %bitcast.20), custom_call_target="tpu_custom_call" | custom-call | tf_op jit(solution)/shard_map/combine_part/pallas_call | solution.py:188
  95.1 10.1 %all_to_all.38 = f32[8,8,128]{2,1,0:T(8,128)S(1)} all-to-all(f32[8,8,128]{2,1,0:T(8,128)} %bitcast.29), channel_id=1, replica_groups=mesh['x'=4,'y'=8,'core'=2,'rank'=8] {'y'}, dimensions={0} | all-to-all | bytes 65536 | tf_op jit(solution)/shard_map/all_to_all | solution.py:16
  105.2 14.3 %all_to_all.39 = f32[8,64,128]{2,1,0:T(8,128)} all-to-all(f32[8,64,128]{2,1,0:T(8,128)S(1)} %broadcast_in_dim.20), channel_id=1, replica_groups=mesh['x'=4,'y'=8,'core'=2,'rank'=8] {'x','core'}, dimensions={0} | all-to-all | bytes 524288 | tf_op jit(solution)/shard_map/all_to_all | solution.py:16
  119.5 7.8 %factor_part.1 = (f32[8,2,16,128]{3,2,1,0:T(8,128)}, f32[128,128]{1,0:T(8,128)}, f32[128,128]{1,0:T(8,128)}) custom-call(f32[512,128]{1,0:T(8,128)} %bitcast.16, f32[8,128]{1,0:T(8,128)} %get-tuple-element.12.alpha_ref, f32[8,4,16,128]{3,2,1,0:T(8,128)} %copy-done, f32[256,128]{1,0:T(8,128)} %get-tuple-element.13.owned), custom_call_target="tpu_custom_call" | custom-call | tf_op jit(solution)/shard_map/factor_part/pallas_call | solution.py:276
  127.3 3.4 %all-to-all-start.6 = ((f32[8,2,16,128]{3,2,1,0:T(8,128)}), f32[8,2,16,128]{3,2,1,0:T(8,128)S(1)}, u32[]{:S(2)}, u32[]{:S(2)}) async-start(f32[8,2,16,128]{3,2,1,0:T(8,128)} %get-tuple-element.14), calls=%async_computation.6 | async-start | bytes 262144 | tf_op jit(solution)/shard_map/all_to_all | solution.py:16
  130.7 2.1 %interface_part.1 = f32[3,16,128]{2,1,0:T(8,128)} custom-call(s32[1]{0:T(128)} %bitcast.14.rank, f32[512,128]{1,0:T(8,128)} %bitcast.17, f32[128,128]{1,0:T(8,128)} %get-tuple-element.16.inverse), custom_call_target="tpu_custom_call" | custom-call | tf_op jit(solution)/shard_map/interface_part/pallas_call | solution.py:288
  132.9 5.5 %all-to-all-done.6 = f32[8,2,16,128]{3,2,1,0:T(8,128)S(1)} async-done(((f32[8,2,16,128]{3,2,1,0:T(8,128)}), f32[8,2,16,128]{3,2,1,0:T(8,128)S(1)}, u32[]{:S(2)}, u32[]{:S(2)}) %all-to-all-start.6) | async-done | bytes 131104 | tf_op jit(solution)/shard_map/all_to_all | solution.py:16
  138.4 0.7 copy.13
  (10 shorter events, 0.1 us)
Async XLA Ops:
  2.3 11.0 %copy-start.3 = (f32[3,3,3,16]{3,2,1,0:T(4,128)S(1)}, f32[3,3,3,16]{3,2,1,0:T(4,128)}, u32[]{:S(2)}) copy-start(f32[3,3,3,16]{3,2,1,0:T(4,128)} %param.9) | copy-start | bytes 5188
  2.3 21.5 %all-to-all-start = ((f32[8,4,16,128]{3,2,1,0:T(8,128)}), f32[8,4,16,128]{3,2,1,0:T(8,128)S(1)}, u32[]{:S(2)}, u32[]{:S(2)}) async-start(f32[8,4,16,128]{3,2,1,0:T(8,128)} %pad_maximum_fusion), calls=%async_computation | async-start | bytes 524288 | tf_op jit(solution)/shard_map/all_to_all | solution.py:16
  23.8 0.7 copy-start
  24.7 6.6 %collective-permute-start.1 = (f32[416,128]{1,0:T(8,128)S(1)}, f32[416,128]{1,0:T(8,128)S(1)}, u32[]{:S(2)}, u32[]{:S(2)}) collective-permute-start(f32[416,128]{1,0:T(8,128)S(1)} %get-tuple-element.23), channel_id=1, source_target_pairs={{1,0},{2,1},{3,2},{4,3},{5,4},{6,5},{7,6},{8,7},{9,8},{10,9},{11,1... | collective-permute-start | bytes 638984 | tf_op jit(solution)/shard_map/ppermute | solution.py:323
  27.0 8.4 %collective-permute-start = (f32[416,128]{1,0:T(8,128)S(1)}, f32[416,128]{1,0:T(8,128)S(1)}, u32[]{:S(2)}, u32[]{:S(2)}) collective-permute-start(f32[416,128]{1,0:T(8,128)S(1)} %get-tuple-element.24), channel_id=1, source_target_pairs={{0,1},{1,2},{2,3},{3,4},{4,5},{5,6},{6,7},{7,8},{8,9},{9,10},{10,1... | collective-permute-start | bytes 638984 | tf_op jit(solution)/shard_map/ppermute | solution.py:322
  31.3 4.8 %copy-start.1 = (f32[416,128]{1,0:T(8,128)}, f32[416,128]{1,0:T(8,128)S(1)}, u32[]{:S(2)}) copy-start(f32[416,128]{1,0:T(8,128)S(1)} %collective-permute-done.1.high) | copy-start | bytes 638980
  35.4 0.7 copy-start.2
  127.3 11.0 %all-to-all-start.6 = ((f32[8,2,16,128]{3,2,1,0:T(8,128)}), f32[8,2,16,128]{3,2,1,0:T(8,128)S(1)}, u32[]{:S(2)}, u32[]{:S(2)}) async-start(f32[8,2,16,128]{3,2,1,0:T(8,128)} %get-tuple-element.14), calls=%async_computation.6 | async-start | bytes 262144 | tf_op jit(solution)/shard_map/all_to_all | solution.py:16

commit v2 on v1

--- a/solution.py
+++ b/solution.py
@@ -35,14 +35,14 @@
 
 
 def local_kernel(
-    mine, low, high, table, left_ref, right_ref, blocks, owned, terms, mixed, coupled, moved, pair
+    mine, low, high, ahead, behind, left_ref, right_ref, blocks, owned, terms, mixed, coupled, moved, pair
 ):
     def slot(index):
         return mine[:, index].reshape(W, W)
 
     fields = [low[0:W], low[W : 2 * W], slot(0), slot(1), high[0:W], high[W : 2 * W]]
     sources = [low[2 * W : 3 * W], slot(2), slot(3), high[2 * W : 3 * W]]
-    weights = [(low, 3 * W), (table, 0), (table, 32), (high, 3 * W)]
+    weights = [(low, 3 * W), (behind, 3 * W), (ahead, 3 * W), (high, 3 * W)]
     right_rows = right_ref[...].reshape(3 * W, W)
     left_rows = left_ref[...].reshape(3 * W, W)
     left_lanes = jnp.concatenate([left_ref[0], left_ref[1], left_ref[2]], axis=1)
@@ -141,7 +141,7 @@
         blocks[pl.ds(8 * version + 7, HALF, stride=24), :] = extra
 
 
-def local_part(mine, low, high, table, left_interface, right_interface):
+def local_part(mine, low, high, ahead, behind, left_interface, right_interface):
     vmem = pl.BlockSpec(memory_space=pltpu.VMEM)
     return pl.pallas_call(
         local_kernel,
@@ -149,7 +149,7 @@
             jax.ShapeDtypeStruct((HALF * 24, W), jnp.float32),
             jax.ShapeDtypeStruct((2 * W, W), jnp.float32),
         ),
-        in_specs=[vmem] * 6,
+        in_specs=[vmem] * 7,
         out_specs=(vmem, vmem),
         scratch_shapes=[
             pltpu.VMEM((6, 3 * W, W), jnp.float32),
@@ -159,36 +159,31 @@
             pltpu.VMEM((8, W, W), jnp.float32),
         ],
         name="local_part",
-    )(mine, low, high, table, left_interface, right_interface)
-
-
-def combine_kernel(got, out, alpha_ref, *, ranks, scale):
-    parts = []
-    for version in range(3):
-        total = got[8 * version : 8 * version + 8]
-        for source in range(1, ranks):
-            total = total + got[24 * source + 8 * version : 24 * source + 8 * version + 8]
-        parts.append(total)
-    row, lane = iotas((8, W))
-    along = jnp.sum(jnp.where((row == 7) & (lane == 1), parts[0], 0.0), keepdims=True)
-    energy = jnp.sum(jnp.where((row == 7) & (lane == 2), parts[0], 0.0), keepdims=True)
-    alpha = jnp.broadcast_to(along, (8, W)) / jnp.broadcast_to(energy, (8, W))
-    alpha_ref[...] = alpha
+    )(mine, low, high, ahead, behind, left_interface, right_interface)
+
+
+def combine_kernel(got, out, alpha_ref, *, scale):
+    count = got.shape[0] // 4
+    parts = [jnp.sum(got[pl.ds(v, count, stride=4), :], axis=0, keepdims=True) for v in range(4)]
+    lane = lax.broadcasted_iota(jnp.int32, (1, W), 1)
+    along = jnp.sum(jnp.where(lane == 1, parts[3], 0.0), axis=1, keepdims=True)
+    energy = jnp.sum(jnp.where(lane == 2, parts[3], 0.0), axis=1, keepdims=True)
+    alpha = jnp.broadcast_to(along, (1, W)) / jnp.broadcast_to(energy, (1, W))
+    alpha_ref[...] = jnp.broadcast_to(alpha, (8, W))
     block = (parts[0] + alpha * (parts[1] + alpha * parts[2])) * scale
-    for m in range(8):
-        out[8 * m : 8 * m + 8] = block
-
-
-def combine_part(got, ranks, scale):
+    out[...] = jnp.broadcast_to(block, out.shape)
+
+
+def combine_part(got, scale):
     vmem = pl.BlockSpec(memory_space=pltpu.VMEM)
 
     def kernel(*refs):
-        combine_kernel(*refs, ranks=ranks, scale=scale)
+        combine_kernel(*refs, scale=scale)
 
     return pl.pallas_call(
         kernel,
         out_shape=(
-            jax.ShapeDtypeStruct((8 * 8, W), jnp.float32),
+            jax.ShapeDtypeStruct((got.shape[0] // 4, W), jnp.float32),
             jax.ShapeDtypeStruct((8, W), jnp.float32),
         ),
         in_specs=[vmem],
@@ -226,15 +221,17 @@
             pivot = jnp.broadcast_to(columns[k][k : k + 1, :], (SIZE, W))
             root = lax.rsqrt(pivot)
             root = root * (1.5 - 0.5 * pivot * (root * root))
-            factor = columns[k] * root
-
-            def eliminate(value):
-                scaled = jnp.broadcast_to(value[k : k + 1, :], (SIZE, W)) * root
-                return jnp.where(sub == k, scaled, jnp.where(sub > k, value - factor * scaled, value))
-
-            left, right = eliminate(left), eliminate(right)
+            factor = jnp.where(sub > k, columns[k] * (root * root), 0.0)
+
+            def spread(value):
+                return jnp.broadcast_to(value[k : k + 1, :], (SIZE, W))
+
             for j in range(k + 1, SIZE):
-                columns[j] = eliminate(columns[j])
+                columns[j] = columns[j] - factor * spread(columns[j])
+            head = spread(left)
+            left = jnp.where(sub == k, head * root, left - factor * head)
+            head = spread(right)
+            right = jnp.where(sub == k, head * root, right - factor * head)
         left = jnp.where(across >= sub + first, left, 0.0)
         triangle[first:last, :] = left
         inverse[first:last, :] = right
@@ -319,15 +316,18 @@
         parts = [mine[:, slot].reshape(width, width) for slot in (0, 1, source)]
         return jnp.concatenate(parts + [table[32 * column : 32 * column + 32]], axis=0)
 
-    low = lax.ppermute(parcel(3, 1), ("x", "y", "core", "rank"), forward)
-    high = lax.ppermute(parcel(2, 0), ("x", "y", "core", "rank"), backward)
-    blocks, owned = local_part(mine, low, high, table, left_interface, right_interface)
+    ahead, behind = parcel(3, 1), parcel(2, 0)
+    low = lax.ppermute(ahead, ("x", "y", "core", "rank"), forward)
+    high = lax.ppermute(behind, ("x", "y", "core", "rank"), backward)
+    blocks, owned = local_part(mine, low, high, ahead, behind, left_interface, right_interface)
 
     block = jnp.sum(exchange(blocks.reshape(8, 192, width), ("x", "core")), axis=0)
-    block = jnp.sum(exchange(block.reshape(8, 24, width), "y"), axis=0)
-    block = exchange(jnp.broadcast_to(block, (ranks, 24, width)), "rank")
-    block, alpha = combine_part(block.reshape(ranks * 24, width), ranks, scale)
-    block = exchange(block.reshape(8, 8, width), "y").reshape(64, width)
+    block = block.reshape(8, 3, 8, width)
+    sums = jnp.broadcast_to(block[:1, :1, 7:, :], (8, 8, 1, width))
+    block = jnp.concatenate([block.transpose(0, 2, 1, 3), sums], axis=2)
+    block = exchange(block.reshape(64, 4, width), ("y", "rank")).reshape(256, width)
+    block, alpha = combine_part(block, scale)
+    block = exchange(block.reshape(64, 1, width), ("y", "rank")).reshape(64, width)
     whole = exchange(jnp.broadcast_to(block, (8, 64, width)), ("x", "core"))
 
     rank = jnp.full((1,), rank_index, jnp.int32)

time: 140 us -> 139 us (level)
    all_to_all x5 -> x4, blocking collectives: 69.7 us -> 69.1 us  [exchange(): return lax.all_to_all(blocks, axis, 0, 0, tiled=True)]
where the time goes in v2:
time: 139 us
  blocking collectives  69.1 us (50%)
  Pallas kernels  23.7 us (17%)
  waiting for transfers between devices  21.1 us (15%)
  starting transfers between devices  19.6 us (14%)
  local copies, waits for them, and re-layouts  2.44 us (2%)
  other arithmetic  1.92 us (1%)
    all_to_all x4, blocking collectives, exchange(): return lax.all_to_all(blocks, axis, 0, 0, tiled=True)  69.1 us
    all_to_all x2, waiting for transfers between devices, exchange(): return lax.all_to_all(blocks, axis, 0, 0, tiled=True)  15.7 us
    all_to_all x2, starting transfers between devices, exchange(): return lax.all_to_all(blocks, axis, 0, 0, tiled=True)  14.4 us
    pallas_call x1, Pallas kernels, local_part(): pl.pallas_call(local_kernel, out_shape=(jax.ShapeDtypeStruct((HALF * 24,...  12.1 us
    pallas_call x1, Pallas kernels, final_part(): pl.pallas_call(factor_kernel, out_shape=(jax.ShapeDtypeStruct((ranks, 2,...  7.81 us
    ppermute x1, waiting for transfers between devices, shards(): low = lax.ppermute(ahead, ('x', 'y', 'core', 'rank'), forward)  4.1 us
    ppermute x1, starting transfers between devices, shards(): low = lax.ppermute(ahead, ('x', 'y', 'core', 'rank'), forward)  2.97 us
  transfers between devices with their start and end apart: 4, of which 4 were waited for; matrix products, arithmetic and copies ran while one was open for 0% of the time, Pallas kernels for 2%

profile of v2, /device:TPU:1, one launch (start us, length us, event | category | flops | bytes accessed | tf_op | source)
XLA Modules:
  0.0 138.6 jit_solution(15322732628172729113)
XLA Ops:
  0.6 1.7 %pad_maximum_fusion = f32[8,4,16,128]{3,2,1,0:T(8,128)} fusion(f32[8,2,16,128]{3,2,1,0:T(8,128)} %bitcast.36, f32[8,2,16,128]{3,2,1,0:T(8,128)} %bitcast.37), kind=kLoop, calls=%fused_computation | loop fusion | flops 65536 | bytes 524288 | tf_op jit(solution)/shard_map/concatenate | solution.py:307
  2.3 0.0 copy-start.5
  2.3 11.0 %all-to-all-start = ((f32[8,4,16,128]{3,2,1,0:T(8,128)}), f32[8,4,16,128]{3,2,1,0:T(8,128)S(1)}, u32[]{:S(2)}, u32[]{:S(2)}) async-start(f32[8,4,16,128]{3,2,1,0:T(8,128)} %pad_maximum_fusion), calls=%async_computation | async-start | bytes 524288 | tf_op jit(solution)/shard_map/all_to_all | solution.py:16
  13.3 0.0 copy-done.5
  13.3 0.1 constant_dynamic-slice_fusion
  13.4 0.2 slice_reduce_fusion
  13.6 10.2 %all-to-all-done.mine = f32[8,4,16,128]{3,2,1,0:T(8,128)S(1)} async-done(((f32[8,4,16,128]{3,2,1,0:T(8,128)}), f32[8,4,16,128]{3,2,1,0:T(8,128)S(1)}, u32[]{:S(2)}, u32[]{:S(2)}) %all-to-all-start) | async-done | bytes 262176 | tf_op jit(solution)/shard_map/all_to_all | solution.py:16
  23.8 0.7 copy-done
  24.5 0.2 fusion.1
  24.7 0.0 copy-start.1
  24.7 0.0 copy-start.2
  24.7 2.3 %collective-permute-start.1 = (f32[416,128]{1,0:T(8,128)S(1)}, f32[416,128]{1,0:T(8,128)S(1)}, u32[]{:S(2)}, u32[]{:S(2)}) collective-permute-start(f32[416,128]{1,0:T(8,128)S(1)} %get-tuple-element.23.behind), channel_id=1, source_target_pairs={{1,0},{2,1},{3,2},{4,3},{5,4},{6,5},{7,6},{8,7},{9,8},{10,9},{11,1... | collective-permute-start | bytes 638984 | tf_op jit(solution)/shard_map/ppermute | solution.py:321
  27.0 3.0 %collective-permute-start = (f32[416,128]{1,0:T(8,128)S(1)}, f32[416,128]{1,0:T(8,128)S(1)}, u32[]{:S(2)}, u32[]{:S(2)}) collective-permute-start(f32[416,128]{1,0:T(8,128)S(1)} %get-tuple-element.24.ahead), channel_id=1, source_target_pairs={{0,1},{1,2},{2,3},{3,4},{4,5},{5,6},{6,7},{7,8},{8,9},{9,10},{10,1... | collective-permute-start | bytes 638984 | tf_op jit(solution)/shard_map/ppermute | solution.py:320
  30.0 1.3 collective-permute-done.1.high
  31.3 4.1 %collective-permute-done.low = f32[416,128]{1,0:T(8,128)S(1)} collective-permute-done((f32[416,128]{1,0:T(8,128)S(1)}, f32[416,128]{1,0:T(8,128)S(1)}, u32[]{:S(2)}, u32[]{:S(2)}) %collective-permute-start) | collective-permute-done | bytes 213024 | tf_op jit(solution)/shard_map/ppermute | solution.py:320
  35.4 0.0 copy-done.1
  35.4 0.0 copy-done.2
  35.4 0.0 copy-done.3
  35.4 0.0 copy-start.4
  35.4 0.7 copy-done.4
  36.1 12.1 %local_part.1 = (f32[1536,128]{1,0:T(8,128)}, f32[256,128]{1,0:T(8,128)}) custom-call(f32[8,4,16,128]{3,2,1,0:T(8,128)} %copy-done, f32[416,128]{1,0:T(8,128)} %copy-done.4, f32[416,128]{1,0:T(8,128)} %copy-done.3, f32[416,128]{1,0:T(8,128)} %copy-done.2, f32[416,128]{1,0:T(8,128)} %copy-done.1, f32[3,128,128]{2,1,0:T(8,128)} %left_ref.1, ...), custom_call_target="tpu_custom_call" | custom-call | tf_op jit(solution)/shard_map/local_part/pallas_call | solution.py:146
  48.2 21.4 %all_to_all.30 = f32[8,192,128]{2,1,0:T(8,128)S(1)} all-to-all(f32[8,192,128]{2,1,0:T(8,128)} %bitcast.26), channel_id=1, replica_groups=mesh['x'=4,'y'=8,'core'=2,'rank'=8] {'x','core'}, dimensions={0} | all-to-all | bytes 1572864 | tf_op jit(solution)/shard_map/all_to_all | solution.py:16
  69.6 0.1 copy.13
  69.7 19.2 %all_to_all.31 = f32[64,4,128]{2,1,0:T(4,128)} all-to-all(f32[64,4,128]{2,1,0:T(4,128)S(1)} %copy.13), channel_id=1, replica_groups=mesh['x'=4,'y'=8,'core'=2,'rank'=8] {'y','rank'}, dimensions={0} | all-to-all | bytes 262144 | tf_op jit(solution)/shard_map/all_to_all | solution.py:16
  88.9 1.6 %combine_part.1 = (f32[64,128]{1,0:T(8,128)}, f32[8,128]{1,0:T(8,128)}) custom-call(f32[256,128]{1,0:T(8,128)} %bitcast.28), custom_call_target="tpu_custom_call" | custom-call | tf_op jit(solution)/shard_map/combine_part/pallas_call | solution.py:183
  90.5 15.4 %all_to_all.32 = f32[64,1,128]{2,1,0:T(1,128)S(1)} all-to-all(f32[64,1,128]{2,1,0:T(1,128)} %bitcast.38), channel_id=1, replica_groups=mesh['x'=4,'y'=8,'core'=2,'rank'=8] {'y','rank'}, dimensions={0} | all-to-all | bytes 65536 | tf_op jit(solution)/shard_map/all_to_all | solution.py:16
  106.0 13.1 %all_to_all.33 = f32[8,64,128]{2,1,0:T(8,128)} all-to-all(f32[8,64,128]{2,1,0:T(8,128)S(1)} %broadcast_in_dim.19), channel_id=1, replica_groups=mesh['x'=4,'y'=8,'core'=2,'rank'=8] {'x','core'}, dimensions={0} | all-to-all | bytes 524288 | tf_op jit(solution)/shard_map/all_to_all | solution.py:16
  119.1 7.8 %factor_part.1 = (f32[8,2,16,128]{3,2,1,0:T(8,128)}, f32[128,128]{1,0:T(8,128)}, f32[128,128]{1,0:T(8,128)}) custom-call(f32[512,128]{1,0:T(8,128)} %bitcast.24, f32[8,128]{1,0:T(8,128)} %get-tuple-element.12.alpha_ref, f32[8,4,16,128]{3,2,1,0:T(8,128)} %copy-done, f32[256,128]{1,0:T(8,128)} %get-tuple-element.13.owned), custom_call_target="tpu_custom_call" | custom-call | tf_op jit(solution)/shard_map/factor_part/pallas_call | solution.py:273
  126.9 3.4 %all-to-all-start.5 = ((f32[8,2,16,128]{3,2,1,0:T(8,128)}), f32[8,2,16,128]{3,2,1,0:T(8,128)S(1)}, u32[]{:S(2)}, u32[]{:S(2)}) async-start(f32[8,2,16,128]{3,2,1,0:T(8,128)} %get-tuple-element.14), calls=%async_computation.5 | async-start | bytes 262144 | tf_op jit(solution)/shard_map/all_to_all | solution.py:16
  130.3 2.1 %interface_part.1 = f32[3,16,128]{2,1,0:T(8,128)} custom-call(s32[1]{0:T(128)} %bitcast.18.rank, f32[512,128]{1,0:T(8,128)} %bitcast.25, f32[128,128]{1,0:T(8,128)} %get-tuple-element.16.inverse), custom_call_target="tpu_custom_call" | custom-call | tf_op jit(solution)/shard_map/interface_part/pallas_call | solution.py:285
  132.4 5.5 %all-to-all-done.5 = f32[8,2,16,128]{3,2,1,0:T(8,128)S(1)} async-done(((f32[8,2,16,128]{3,2,1,0:T(8,128)}), f32[8,2,16,128]{3,2,1,0:T(8,128)S(1)}, u32[]{:S(2)}, u32[]{:S(2)}) %all-to-all-start.5) | async-done | bytes 131104 | tf_op jit(solution)/shard_map/all_to_all | solution.py:16
  137.9 0.7 copy.17
  (12 shorter events, 0.1 us)
Async XLA Ops:
  2.3 11.0 %copy-start.5 = (f32[3,3,3,16]{3,2,1,0:T(4,128)S(1)}, f32[3,3,3,16]{3,2,1,0:T(4,128)}, u32[]{:S(2)}) copy-start(f32[3,3,3,16]{3,2,1,0:T(4,128)} %param.9) | copy-start | bytes 5188
  2.3 21.5 %all-to-all-start = ((f32[8,4,16,128]{3,2,1,0:T(8,128)}), f32[8,4,16,128]{3,2,1,0:T(8,128)S(1)}, u32[]{:S(2)}, u32[]{:S(2)}) async-start(f32[8,4,16,128]{3,2,1,0:T(8,128)} %pad_maximum_fusion), calls=%async_computation | async-start | bytes 524288 | tf_op jit(solution)/shard_map/all_to_all | solution.py:16
  23.8 0.7 copy-start
  24.7 10.7 %copy-start.1 = (f32[416,128]{1,0:T(8,128)}, f32[416,128]{1,0:T(8,128)S(1)}, u32[]{:S(2)}) copy-start(f32[416,128]{1,0:T(8,128)S(1)} %get-tuple-element.23.behind) | copy-start | bytes 638980
  24.7 10.7 %copy-start.2 = (f32[416,128]{1,0:T(8,128)}, f32[416,128]{1,0:T(8,128)S(1)}, u32[]{:S(2)}) copy-start(f32[416,128]{1,0:T(8,128)S(1)} %get-tuple-element.24.ahead) | copy-start | bytes 638980
  24.7 6.6 %collective-permute-start.1 = (f32[416,128]{1,0:T(8,128)S(1)}, f32[416,128]{1,0:T(8,128)S(1)}, u32[]{:S(2)}, u32[]{:S(2)}) collective-permute-start(f32[416,128]{1,0:T(8,128)S(1)} %get-tuple-element.23.behind), channel_id=1, source_target_pairs={{1,0},{2,1},{3,2},{4,3},{5,4},{6,5},{7,6},{8,7},{9,8},{10,9},{11,1... | collective-permute-start | bytes 638984 | tf_op jit(solution)/shard_map/ppermute | solution.py:321
  27.0 8.4 %collective-permute-start = (f32[416,128]{1,0:T(8,128)S(1)}, f32[416,128]{1,0:T(8,128)S(1)}, u32[]{:S(2)}, u32[]{:S(2)}) collective-permute-start(f32[416,128]{1,0:T(8,128)S(1)} %get-tuple-element.24.ahead), channel_id=1, source_target_pairs={{0,1},{1,2},{2,3},{3,4},{4,5},{5,6},{6,7},{7,8},{8,9},{9,10},{10,1... | collective-permute-start | bytes 638984 | tf_op jit(solution)/shard_map/ppermute | solution.py:320
  31.3 4.1 %copy-start.3 = (f32[416,128]{1,0:T(8,128)}, f32[416,128]{1,0:T(8,128)S(1)}, u32[]{:S(2)}) copy-start(f32[416,128]{1,0:T(8,128)S(1)} %collective-permute-done.1.high) | copy-start | bytes 638980
  35.4 0.7 copy-start.4
  126.9 11.0 %all-to-all-start.5 = ((f32[8,2,16,128]{3,2,1,0:T(8,128)}), f32[8,2,16,128]{3,2,1,0:T(8,128)S(1)}, u32[]{:S(2)}, u32[]{:S(2)}) async-start(f32[8,2,16,128]{3,2,1,0:T(8,128)} %get-tuple-element.14), calls=%async_computation.5 | async-start | bytes 262144 | tf_op jit(solution)/shard_map/all_to_all | solution.py:16

commit v3 on v2

--- a/solution.py
+++ b/solution.py
@@ -30,6 +30,20 @@
     )
 
 
+def halves(value):
+    high = value.astype(jnp.bfloat16)
+    return high, (value - high.astype(jnp.float32)).astype(jnp.bfloat16)
+
+
+def split_product(left, right, contract):
+    def one(a, b):
+        return lax.dot_general(
+            a, b, (((1,), (contract,)), ((), ())), preferred_element_type=jnp.float32
+        )
+
+    return one(left[0], right[0]) + (one(left[0], right[1]) + one(left[1], right[0]))
+
+
 def iotas(shape):
     return lax.broadcasted_iota(jnp.int32, shape, 0), lax.broadcasted_iota(jnp.int32, shape, 1)
 
@@ -43,13 +57,13 @@
     fields = [low[0:W], low[W : 2 * W], slot(0), slot(1), high[0:W], high[W : 2 * W]]
     sources = [low[2 * W : 3 * W], slot(2), slot(3), high[2 * W : 3 * W]]
     weights = [(low, 3 * W), (behind, 3 * W), (ahead, 3 * W), (high, 3 * W)]
-    right_rows = right_ref[...].reshape(3 * W, W)
-    left_rows = left_ref[...].reshape(3 * W, W)
-    left_lanes = jnp.concatenate([left_ref[0], left_ref[1], left_ref[2]], axis=1)
+    right_rows = halves(right_ref[...].reshape(3 * W, W))
+    left_rows = halves(left_ref[...].reshape(3 * W, W))
+    left_lanes = halves(jnp.concatenate([left_ref[0], left_ref[1], left_ref[2]], axis=1))
 
     def contract(values):
         for k in range(0, len(values), 2):
-            both = product(right_rows, jnp.concatenate(values[k : k + 2], axis=1))
+            both = split_product(right_rows, halves(jnp.concatenate(values[k : k + 2], axis=1)), 0)
             terms[k] = both[:, :W]
             terms[k + 1] = both[:, W:]
 
@@ -74,7 +88,7 @@
             return carry
 
         lax.fori_loop(0, W // 8, step, 0, unroll=2)
-        return product_t(coupled[...], left_lanes)
+        return split_product(halves(coupled[...]), left_lanes, 1)
 
     contract(fields)
     residual = [sources[i] - couple(weights[i], i) for i in range(4)]
@@ -93,7 +107,9 @@
 
     for u in range(2):
         stack = pair[4 * u : 4 * u + 4].reshape(4 * W, W)
-        mixed[4 * u : 4 * u + 4] = product_t(stack, left_rows).reshape(4, W, 3 * W)
+        mixed[4 * u : 4 * u + 4] = split_product(halves(stack), left_rows, 1).reshape(
+            4, W, 3 * W
+        )
     for i in range(2):
         cs = rows_of(weights[1 + i])
 
@@ -120,7 +136,8 @@
         ],
         axis=0,
     )
-    forms = [product_t(moved[u], both) for u in range(2)]
+    split = halves(both)
+    forms = [split_product(halves(moved[u]), split, 1) for u in range(2)]
     tables = [forms[0][:, :W], forms[0][:, W:] + forms[1][:, :W], forms[1][:, W:]]
     square = product_t(both, both)
     grams = [square[:W, :W], square[:W, W:] + square[W:, :W], square[W:, W:]]
@@ -141,13 +158,17 @@
         blocks[pl.ds(8 * version + 7, HALF, stride=24), :] = extra
 
 
+def near(*values):
+    return [pltpu.with_memory_space_constraint(value, pltpu.VMEM) for value in values]
+
+
 def local_part(mine, low, high, ahead, behind, left_interface, right_interface):
     vmem = pl.BlockSpec(memory_space=pltpu.VMEM)
     return pl.pallas_call(
         local_kernel,
         out_shape=(
-            jax.ShapeDtypeStruct((HALF * 24, W), jnp.float32),
-            jax.ShapeDtypeStruct((2 * W, W), jnp.float32),
+            pltpu.VMEM((HALF * 24, W), jnp.float32),
+            pltpu.VMEM((2 * W, W), jnp.float32),
         ),
         in_specs=[vmem] * 7,
         out_specs=(vmem, vmem),
@@ -159,7 +180,7 @@
             pltpu.VMEM((8, W, W), jnp.float32),
         ],
         name="local_part",
-    )(mine, low, high, ahead, behind, left_interface, right_interface)
+    )(*near(mine, low, high, ahead, behind), left_interface, right_interface)
 
 
 def combine_kernel(got, out, alpha_ref, *, scale):
@@ -183,13 +204,13 @@
     return pl.pallas_call(
         kernel,
         out_shape=(
-            jax.ShapeDtypeStruct((got.shape[0] // 4, W), jnp.float32),
-            jax.ShapeDtypeStruct((8, W), jnp.float32),
+            pltpu.VMEM((got.shape[0] // 4, W), jnp.float32),
+            pltpu.VMEM((8, W), jnp.float32),
         ),
         in_specs=[vmem],
         out_specs=(vmem, vmem),
         name="combine_part",
-    )(got)
+    )(*near(got))
 
 
 def factor_kernel(whole, alpha_ref, mine, owned, basis, triangle, inverse, table):
@@ -273,22 +294,22 @@
     basis, triangle, inverse = pl.pallas_call(
         factor_kernel,
         out_shape=(
-            jax.ShapeDtypeStruct((ranks, 2, piece, W), jnp.float32),
+            pltpu.VMEM((ranks, 2, piece, W), jnp.float32),
             jax.ShapeDtypeStruct((W, W), jnp.float32),
-            jax.ShapeDtypeStruct((W, W), jnp.float32),
+            pltpu.VMEM((W, W), jnp.float32),
         ),
         in_specs=[vmem] * 4,
         out_specs=(vmem,) * 3,
         scratch_shapes=[pltpu.VMEM((W, 2 * W), jnp.float32)],
         name="factor_part",
-    )(whole, alpha, mine, owned)
+    )(*near(whole, alpha, mine, owned))
     interface = pl.pallas_call(
         interface_kernel,
         out_shape=jax.ShapeDtypeStruct((3, piece, W), jnp.float32),
         in_specs=[pl.BlockSpec(memory_space=pltpu.SMEM), vmem, vmem],
         out_specs=vmem,
         name="interface_part",
-    )(rank, whole, inverse)
+    )(rank, *near(whole, inverse))
     return basis, triangle, interface
 
 

time: 139 us -> 129 us (0.928)
  Pallas kernels: 23.7 us -> 15.7 us
  blocking collectives: 69.1 us -> 67.3 us
    pallas_call x3, Pallas kernels: 21.5 us -> 14.6 us  [the longest x1 7.72 us: local_part(): pl.pallas_call(local_kernel, out_shape=(pltpu.VMEM((HALF * 24, W), jnp.fl...]
    all_to_all x4, blocking collectives: 69.1 us -> 67.3 us  [exchange(): return lax.all_to_all(blocks, axis, 0, 0, tiled=True)]
  transfers between devices with their start and end apart: 4 -> 4, of which waited for: 4 -> 4; matrix products, arithmetic and copies ran while one was open for 0% -> 0% of each run, Pallas kernels for 2% -> 1%
where the time goes in v3:
time: 129 us; the launch traced here: 128 us
  blocking collectives  67.3 us (52%)
  waiting for transfers between devices  22.1 us (17%)
  starting transfers between devices  19.6 us (15%)
  Pallas kernels  15.7 us (12%)
  other arithmetic  1.91 us (1%)
    all_to_all x4, blocking collectives, exchange(): return lax.all_to_all(blocks, axis, 0, 0, tiled=True)  67.3 us
    all_to_all x2, waiting for transfers between devices, exchange(): return lax.all_to_all(blocks, axis, 0, 0, tiled=True)  16.7 us
    all_to_all x2, starting transfers between devices, exchange(): return lax.all_to_all(blocks, axis, 0, 0, tiled=True)  14.4 us
    pallas_call x1, Pallas kernels, local_part(): pl.pallas_call(local_kernel, out_shape=(pltpu.VMEM((HALF * 24, W), jnp.fl...  7.72 us
    pallas_call x1, Pallas kernels, final_part(): pl.pallas_call(factor_kernel, out_shape=(pltpu.VMEM((ranks, 2, piece, W),...  6.74 us
    ppermute x1, waiting for transfers between devices, shards(): low = lax.ppermute(ahead, ('x', 'y', 'core', 'rank'), forward)  4.1 us
    ppermute x1, starting transfers between devices, shards(): low = lax.ppermute(ahead, ('x', 'y', 'core', 'rank'), forward)  2.97 us
  transfers between devices with their start and end apart: 4, of which 4 were waited for; matrix products, arithmetic and copies ran while one was open for 0% of the time, Pallas kernels for 1%

profile of v3, /device:TPU:1, one launch (start us, length us, event | category | flops | bytes accessed | tf_op | source)
XLA Modules:
  0.0 128.5 jit_solution(13396402463886450164)
XLA Ops:
  0.6 1.7 %pad_maximum_fusion = f32[8,4,16,128]{3,2,1,0:T(8,128)} fusion(f32[8,2,16,128]{3,2,1,0:T(8,128)} %bitcast.37, f32[8,2,16,128]{3,2,1,0:T(8,128)} %bitcast.38), kind=kLoop, calls=%fused_computation | loop fusion | flops 65536 | bytes 524288 | tf_op jit(solution)/shard_map/concatenate | solution.py:328
  2.3 0.0 copy-start
  2.3 11.0 %all-to-all-start = ((f32[8,4,16,128]{3,2,1,0:T(8,128)}), f32[8,4,16,128]{3,2,1,0:T(8,128)S(1)}, u32[]{:S(2)}, u32[]{:S(2)}) async-start(f32[8,4,16,128]{3,2,1,0:T(8,128)} %pad_maximum_fusion), calls=%async_computation | async-start | bytes 524288 | tf_op jit(solution)/shard_map/all_to_all | solution.py:16
  13.3 0.0 copy-done
  13.3 0.1 constant_dynamic-slice_fusion
  13.4 0.2 slice_reduce_fusion
  13.6 10.2 %all-to-all-done.mine = f32[8,4,16,128]{3,2,1,0:T(8,128)S(1)} async-done(((f32[8,4,16,128]{3,2,1,0:T(8,128)}), f32[8,4,16,128]{3,2,1,0:T(8,128)S(1)}, u32[]{:S(2)}, u32[]{:S(2)}) %all-to-all-start) | async-done | bytes 262176 | tf_op jit(solution)/shard_map/all_to_all | solution.py:16
  23.8 0.2 fusion.1
  24.0 2.3 %collective-permute-start.1 = (f32[416,128]{1,0:T(8,128)S(1)}, f32[416,128]{1,0:T(8,128)S(1)}, u32[]{:S(2)}, u32[]{:S(2)}) collective-permute-start(f32[416,128]{1,0:T(8,128)S(1)} %get-tuple-element.23.behind), channel_id=1, source_target_pairs={{1,0},{2,1},{3,2},{4,3},{5,4},{6,5},{7,6},{8,7},{9,8},{10,9},{11,1... | collective-permute-start | bytes 638984 | tf_op jit(solution)/shard_map/ppermute | solution.py:342
  26.3 3.0 %collective-permute-start = (f32[416,128]{1,0:T(8,128)S(1)}, f32[416,128]{1,0:T(8,128)S(1)}, u32[]{:S(2)}, u32[]{:S(2)}) collective-permute-start(f32[416,128]{1,0:T(8,128)S(1)} %get-tuple-element.24.ahead), channel_id=1, source_target_pairs={{0,1},{1,2},{2,3},{3,4},{4,5},{5,6},{6,7},{7,8},{8,9},{9,10},{10,1... | collective-permute-start | bytes 638984 | tf_op jit(solution)/shard_map/ppermute | solution.py:341
  29.3 1.3 %collective-permute-done.1.high = f32[416,128]{1,0:T(8,128)S(1)} collective-permute-done((f32[416,128]{1,0:T(8,128)S(1)}, f32[416,128]{1,0:T(8,128)S(1)}, u32[]{:S(2)}, u32[]{:S(2)}) %collective-permute-start.1) | collective-permute-done | bytes 213024 | tf_op jit(solution)/shard_map/ppermute | solution.py:342
  30.6 4.1 %collective-permute-done.low = f32[416,128]{1,0:T(8,128)S(1)} collective-permute-done((f32[416,128]{1,0:T(8,128)S(1)}, f32[416,128]{1,0:T(8,128)S(1)}, u32[]{:S(2)}, u32[]{:S(2)}) %collective-permute-start) | collective-permute-done | bytes 213024 | tf_op jit(solution)/shard_map/ppermute | solution.py:341
  34.7 7.7 %local_part.1 = (f32[1536,128]{1,0:T(8,128)S(1)}, f32[256,128]{1,0:T(8,128)S(1)}) custom-call(f32[8,4,16,128]{3,2,1,0:T(8,128)S(1)} %all-to-all-done.mine, f32[416,128]{1,0:T(8,128)S(1)} %collective-permute-done.low, f32[416,128]{1,0:T(8,128)S(1)} %collective-permute-done.1.high, f32[416,128]{1,0:T(8,128)S(1)} %get-tuple-element.24.ahead, ...), custom_call_target="tpu_custom_call" | custom-call | tf_op jit(solution)/shard_map/local_part/pallas_call | solution.py:167
  42.4 21.2 %all_to_all.30 = f32[8,192,128]{2,1,0:T(8,128)S(1)} all-to-all(f32[8,192,128]{2,1,0:T(8,128)S(1)} %bitcast.26), channel_id=1, replica_groups=mesh['x'=4,'y'=8,'core'=2,'rank'=8] {'x','core'}, dimensions={0} | all-to-all | bytes 1572864 | tf_op jit(solution)/shard_map/all_to_all | solution.py:16
  63.7 0.1 copy.13
  63.8 19.1 %all_to_all.31 = f32[64,4,128]{2,1,0:T(4,128)S(1)} all-to-all(f32[64,4,128]{2,1,0:T(4,128)S(1)} %copy.13), channel_id=1, replica_groups=mesh['x'=4,'y'=8,'core'=2,'rank'=8] {'y','rank'}, dimensions={0} | all-to-all | bytes 262144 | tf_op jit(solution)/shard_map/all_to_all | solution.py:16
  82.8 0.1 combine_part.1
  82.9 14.6 %all_to_all.32 = f32[64,1,128]{2,1,0:T(1,128)S(1)} all-to-all(f32[64,1,128]{2,1,0:T(1,128)S(1)} %bitcast.28), channel_id=1, replica_groups=mesh['x'=4,'y'=8,'core'=2,'rank'=8] {'y','rank'}, dimensions={0} | all-to-all | bytes 65536 | tf_op jit(solution)/shard_map/all_to_all | solution.py:16
  97.6 12.4 %all_to_all.33 = f32[8,64,128]{2,1,0:T(8,128)S(1)} all-to-all(f32[8,64,128]{2,1,0:T(8,128)S(1)} %broadcast_in_dim.19), channel_id=1, replica_groups=mesh['x'=4,'y'=8,'core'=2,'rank'=8] {'x','core'}, dimensions={0} | all-to-all | bytes 524288 | tf_op jit(solution)/shard_map/all_to_all | solution.py:16
  110.0 6.7 %factor_part.1 = (f32[8,2,16,128]{3,2,1,0:T(8,128)}, f32[128,128]{1,0:T(8,128)}, f32[128,128]{1,0:T(8,128)S(1)}) custom-call(f32[512,128]{1,0:T(8,128)S(1)} %bitcast.24, f32[8,128]{1,0:T(8,128)S(1)} %get-tuple-element.12.alpha_ref, f32[8,4,16,128]{3,2,1,0:T(8,128)S(1)} %all-to-all-done.mine, f32[256,128]{1,0:T(8,128)S(1)} %get-tuple-element.13.owned), custom_call_target="tpu_custom_call" | custom-call | tf_op jit(solution)/shard_map/factor_part/pallas_call | solution.py:294
  116.8 3.4 %all-to-all-start.5 = ((f32[8,2,16,128]{3,2,1,0:T(8,128)}), f32[8,2,16,128]{3,2,1,0:T(8,128)S(1)}, u32[]{:S(2)}, u32[]{:S(2)}) async-start(f32[8,2,16,128]{3,2,1,0:T(8,128)} %get-tuple-element.14), calls=%async_computation.5 | async-start | bytes 262144 | tf_op jit(solution)/shard_map/all_to_all | solution.py:16
  120.2 1.2 interface_part.1
  121.3 6.5 %all-to-all-done.5 = f32[8,2,16,128]{3,2,1,0:T(8,128)S(1)} async-done(((f32[8,2,16,128]{3,2,1,0:T(8,128)}), f32[8,2,16,128]{3,2,1,0:T(8,128)S(1)}, u32[]{:S(2)}, u32[]{:S(2)}) %all-to-all-start.5) | async-done | bytes 131104 | tf_op jit(solution)/shard_map/all_to_all | solution.py:16
  127.8 0.7 copy.17
  (10 shorter events, 0.1 us)
Async XLA Ops:
  2.3 11.0 %copy-start = (f32[3,3,3,16]{3,2,1,0:T(4,128)S(1)}, f32[3,3,3,16]{3,2,1,0:T(4,128)}, u32[]{:S(2)}) copy-start(f32[3,3,3,16]{3,2,1,0:T(4,128)} %param.9) | copy-start | bytes 5188
  2.3 21.5 %all-to-all-start = ((f32[8,4,16,128]{3,2,1,0:T(8,128)}), f32[8,4,16,128]{3,2,1,0:T(8,128)S(1)}, u32[]{:S(2)}, u32[]{:S(2)}) async-start(f32[8,4,16,128]{3,2,1,0:T(8,128)} %pad_maximum_fusion), calls=%async_computation | async-start | bytes 524288 | tf_op jit(solution)/shard_map/all_to_all | solution.py:16
  24.0 6.6 %collective-permute-start.1 = (f32[416,128]{1,0:T(8,128)S(1)}, f32[416,128]{1,0:T(8,128)S(1)}, u32[]{:S(2)}, u32[]{:S(2)}) collective-permute-start(f32[416,128]{1,0:T(8,128)S(1)} %get-tuple-element.23.behind), channel_id=1, source_target_pairs={{1,0},{2,1},{3,2},{4,3},{5,4},{6,5},{7,6},{8,7},{9,8},{10,9},{11,1... | collective-permute-start | bytes 638984 | tf_op jit(solution)/shard_map/ppermute | solution.py:342
  26.3 8.4 %collective-permute-start = (f32[416,128]{1,0:T(8,128)S(1)}, f32[416,128]{1,0:T(8,128)S(1)}, u32[]{:S(2)}, u32[]{:S(2)}) collective-permute-start(f32[416,128]{1,0:T(8,128)S(1)} %get-tuple-element.24.ahead), channel_id=1, source_target_pairs={{0,1},{1,2},{2,3},{3,4},{4,5},{5,6},{6,7},{7,8},{8,9},{9,10},{10,1... | collective-permute-start | bytes 638984 | tf_op jit(solution)/shard_map/ppermute | solution.py:341
  116.8 11.0 %all-to-all-start.5 = ((f32[8,2,16,128]{3,2,1,0:T(8,128)}), f32[8,2,16,128]{3,2,1,0:T(8,128)S(1)}, u32[]{:S(2)}, u32[]{:S(2)}) async-start(f32[8,2,16,128]{3,2,1,0:T(8,128)} %get-tuple-element.14), calls=%async_computation.5 | async-start | bytes 262144 | tf_op jit(solution)/shard_map/all_to_all | solution.py:16

commit v4 on v3

--- a/solution.py
+++ b/solution.py
@@ -10,6 +10,7 @@
 W = 128
 HALF = W // 2
 SIZE = 16
+ROOM = 16 * 2**20
 
 
 def exchange(blocks, axis):
@@ -48,86 +49,176 @@
     return lax.broadcasted_iota(jnp.int32, shape, 0), lax.broadcasted_iota(jnp.int32, shape, 1)
 
 
+def near(*values):
+    return [pltpu.with_memory_space_constraint(value, pltpu.VMEM) for value in values]
+
+
+def own_slot(mine, index):
+    return mine[:, index].reshape(W, W)
+
+
+def contract(right_rows, values, terms, first):
+    for k in range(0, len(values), 2):
+        both = split_product(right_rows, halves(jnp.concatenate(values[k : k + 2], axis=1)), 0)
+        terms[first + k] = both[:, :W]
+        terms[first + k + 1] = both[:, W:]
+
+
+def couple(place, sources, target, base, left_first):
+    ref, start = place
+    used = {offset for offset, _ in sources}
+    weight = {
+        (i, j, offset): jnp.broadcast_to(
+            ref[start + i * 9 + j * 3 + offset : start + i * 9 + j * 3 + offset + 1, :], (8, W)
+        )
+        for i in range(3)
+        for j in range(3)
+        for offset in used
+    }
+
+    def step(chunk, carry):
+        at = pl.multiple_of(chunk * 8, 8)
+        sums = [None if base is None else base(index, at) for index in range(3)]
+        for offset, rows in sources:
+            for inner in range(3):
+                value = rows(inner, at)
+                for outer in range(3):
+                    key = (inner, outer) if left_first else (outer, inner)
+                    part = weight[key + (offset,)] * value
+                    sums[outer] = part if sums[outer] is None else sums[outer] + part
+        for index in range(3):
+            target(index, at, sums[index])
+        return carry
+
+    lax.fori_loop(0, W // 8, step, 0, unroll=2)
+
+
+def term_rows(terms, place):
+    return lambda index, at: terms[place, pl.ds(index * W + at, 8), :]
+
+
+def mixed_rows(mixed, place):
+    return lambda index, at: mixed[place, pl.ds(at, 8), index * W : (index + 1) * W]
+
+
+def lanes_of(ref, place):
+    def load(index, at):
+        return ref[place, pl.ds(at, 8), index * W : (index + 1) * W]
+
+    def store(index, at, value):
+        ref[place, pl.ds(at, 8), index * W : (index + 1) * W] = value
+
+    return load, store
+
+
+def moved_of(ref, lead, place):
+    def load(index, at):
+        return ref[lead + (pl.ds(index * W + at, 8), slice(place * W, (place + 1) * W))]
+
+    def store(index, at, value):
+        ref[lead + (pl.ds(index * W + at, 8), slice(place * W, (place + 1) * W))] = value
+
+    return load, store
+
+
+def early_kernel(mine, ahead, behind, left_ref, right_ref, terms, partial, shifted, mixed):
+    right_rows = halves(right_ref[...].reshape(3 * W, W))
+    left_rows = halves(left_ref[...].reshape(3 * W, W))
+    fields = [own_slot(mine, 0), own_slot(mine, 1)]
+    weights = [(behind, 3 * W), (ahead, 3 * W)]
+    contract(right_rows, fields, terms, 0)
+    stack = halves(jnp.concatenate(fields, axis=0))
+    mixed[...] = split_product(stack, left_rows, 1).reshape(2, W, 3 * W)
+    for i in range(2):
+        present = [(1 - i + k, term_rows(terms, k)) for k in range(2)]
+        couple(weights[i], present, lanes_of(partial, i)[1], None, False)
+        present = [(1 - i + k, mixed_rows(mixed, k)) for k in range(2)]
+        couple(weights[i], present, moved_of(shifted, (), i)[1], None, True)
+
+
+def early_part(mine, ahead, behind, left_interface, right_interface):
+    vmem = pl.BlockSpec(memory_space=pltpu.VMEM)
+    return pl.pallas_call(
+        early_kernel,
+        out_shape=(
+            pltpu.VMEM((2, 3 * W, W), jnp.float32),
+            pltpu.VMEM((2, W, 3 * W), jnp.float32),
+            pltpu.VMEM((3 * W, 2 * W), jnp.float32),
+        ),
+        in_specs=[vmem] * 5,
+        out_specs=(vmem,) * 3,
+        scratch_shapes=[pltpu.VMEM((2, W, 3 * W), jnp.float32)],
+        compiler_params=pltpu.CompilerParams(vmem_limit_bytes=ROOM),
+        name="early_part",
+    )(*near(mine, ahead, behind, left_interface, right_interface))
+
+
 def local_kernel(
-    mine, low, high, ahead, behind, left_ref, right_ref, blocks, owned, terms, mixed, coupled, moved, pair
+    mine,
+    low,
+    high,
+    ahead,
+    behind,
+    own_terms,
+    partial,
+    shifted,
+    left_ref,
+    right_ref,
+    blocks,
+    owned,
+    terms,
+    mixed,
+    coupled,
+    moved,
+    pair,
 ):
-    def slot(index):
-        return mine[:, index].reshape(W, W)
-
-    fields = [low[0:W], low[W : 2 * W], slot(0), slot(1), high[0:W], high[W : 2 * W]]
-    sources = [low[2 * W : 3 * W], slot(2), slot(3), high[2 * W : 3 * W]]
+    outer = [low[0:W], low[W : 2 * W], high[0:W], high[W : 2 * W]]
+    sources = [low[2 * W : 3 * W], own_slot(mine, 2), own_slot(mine, 3), high[2 * W : 3 * W]]
     weights = [(low, 3 * W), (behind, 3 * W), (ahead, 3 * W), (high, 3 * W)]
     right_rows = halves(right_ref[...].reshape(3 * W, W))
     left_rows = halves(left_ref[...].reshape(3 * W, W))
     left_lanes = halves(jnp.concatenate([left_ref[0], left_ref[1], left_ref[2]], axis=1))
-
-    def contract(values):
-        for k in range(0, len(values), 2):
-            both = split_product(right_rows, halves(jnp.concatenate(values[k : k + 2], axis=1)), 0)
-            terms[k] = both[:, :W]
-            terms[k + 1] = both[:, W:]
-
-    def rows_of(place):
-        ref, base = place
-        return [jnp.broadcast_to(ref[base + t : base + t + 1, :], (8, W)) for t in range(27)]
-
-    def couple(place, first):
-        cs = rows_of(place)
-
-        def step(chunk, carry):
-            at = pl.multiple_of(chunk * 8, 8)
-            sums = [None] * 3
-            for offset in range(3):
-                for beta in range(3):
-                    value = terms[first + offset, pl.ds(beta * W + at, 8), :]
-                    for alpha in range(3):
-                        part = cs[alpha * 9 + beta * 3 + offset] * value
-                        sums[alpha] = part if sums[alpha] is None else sums[alpha] + part
-            for alpha in range(3):
-                coupled[pl.ds(at, 8), alpha * W : (alpha + 1) * W] = sums[alpha]
-            return carry
-
-        lax.fori_loop(0, W // 8, step, 0, unroll=2)
-        return split_product(halves(coupled[...]), left_lanes, 1)
-
-    contract(fields)
-    residual = [sources[i] - couple(weights[i], i) for i in range(4)]
+    store = lanes_of(coupled, 0)[1]
+
+    def finish():
+        return split_product(halves(coupled[0]), left_lanes, 1)
+
+    contract(right_rows, outer, terms, 0)
+    lists = [
+        [(0, term_rows(terms, 0)), (1, term_rows(terms, 1)), (2, term_rows(own_terms, 0))],
+        [(0, term_rows(terms, 1))],
+        [(2, term_rows(terms, 2))],
+        [(0, term_rows(own_terms, 1)), (1, term_rows(terms, 2)), (2, term_rows(terms, 3))],
+    ]
+    residual = []
     for i in range(4):
-        pair[i] = fields[i + 1]
+        base = lanes_of(partial, i - 1)[0] if i in (1, 2) else None
+        couple(weights[i], lists[i], store, base, False)
+        residual.append(sources[i] - finish())
+    pair[0], pair[3] = outer[1], outer[2]
+    pair[1], pair[2] = own_slot(mine, 0), own_slot(mine, 1)
+    for i in range(4):
         pair[4 + i] = residual[i]
     owned[0:W] = residual[1]
     owned[W : 2 * W] = residual[2]
-    contract(residual)
+    contract(right_rows, residual, terms, 0)
     along = jnp.zeros((1, 1), jnp.float32)
     energy = jnp.zeros((1, 1), jnp.float32)
     for i in range(2):
-        image = couple(weights[1 + i], i)
+        present = [(offset, term_rows(terms, i + offset)) for offset in range(3)]
+        couple(weights[1 + i], present, store, None, False)
+        image = finish()
         along = along + jnp.sum(pair[5 + i] * image, keepdims=True)
         energy = energy + jnp.sum(image * image, keepdims=True)
 
-    for u in range(2):
-        stack = pair[4 * u : 4 * u + 4].reshape(4 * W, W)
-        mixed[4 * u : 4 * u + 4] = split_product(halves(stack), left_rows, 1).reshape(
-            4, W, 3 * W
-        )
+    stack = halves(jnp.concatenate([outer[1], outer[2]] + residual, axis=0))
+    mixed[...] = split_product(stack, left_rows, 1).reshape(6, W, 3 * W)
     for i in range(2):
-        cs = rows_of(weights[1 + i])
-
-        def step(chunk, carry):
-            u = chunk // (W // 8)
-            at = pl.multiple_of((chunk % (W // 8)) * 8, 8)
-            sums = [None] * 3
-            for offset in range(3):
-                for alpha in range(3):
-                    value = mixed[4 * u + i + offset, pl.ds(at, 8), alpha * W : (alpha + 1) * W]
-                    for beta in range(3):
-                        part = cs[alpha * 9 + beta * 3 + offset] * value
-                        sums[beta] = part if sums[beta] is None else sums[beta] + part
-            for beta in range(3):
-                moved[u, pl.ds(beta * W + at, 8), i * W : (i + 1) * W] = sums[beta]
-            return carry
-
-        lax.fori_loop(0, 2 * (W // 8), step, 0, unroll=2)
+        base = moved_of(shifted, (), i)[0]
+        present = [(2 * i, mixed_rows(mixed, i))]
+        couple(weights[1 + i], present, moved_of(moved, (0,), i)[1], base, True)
+        present = [(offset, mixed_rows(mixed, 2 + i + offset)) for offset in range(3)]
+        couple(weights[1 + i], present, moved_of(moved, (1,), i)[1], None, True)
 
     both = jnp.concatenate(
         [
@@ -158,11 +249,7 @@
         blocks[pl.ds(8 * version + 7, HALF, stride=24), :] = extra
 
 
-def near(*values):
-    return [pltpu.with_memory_space_constraint(value, pltpu.VMEM) for value in values]
-
-
-def local_part(mine, low, high, ahead, behind, left_interface, right_interface):
+def local_part(mine, low, high, ahead, behind, early, left_interface, right_interface):
     vmem = pl.BlockSpec(memory_space=pltpu.VMEM)
     return pl.pallas_call(
         local_kernel,
@@ -170,17 +257,18 @@
             pltpu.VMEM((HALF * 24, W), jnp.float32),
             pltpu.VMEM((2 * W, W), jnp.float32),
         ),
-        in_specs=[vmem] * 7,
+        in_specs=[vmem] * 10,
         out_specs=(vmem, vmem),
         scratch_shapes=[
-            pltpu.VMEM((6, 3 * W, W), jnp.float32),
-            pltpu.VMEM((8, W, 3 * W), jnp.float32),
-            pltpu.VMEM((W, 3 * W), jnp.float32),
+            pltpu.VMEM((4, 3 * W, W), jnp.float32),
+            pltpu.VMEM((6, W, 3 * W), jnp.float32),
+            pltpu.VMEM((1, W, 3 * W), jnp.float32),
             pltpu.VMEM((2, 3 * W, 2 * W), jnp.float32),
             pltpu.VMEM((8, W, W), jnp.float32),
         ],
+        compiler_params=pltpu.CompilerParams(vmem_limit_bytes=ROOM),
         name="local_part",
-    )(*near(mine, low, high, ahead, behind), left_interface, right_interface)
+    )(*near(mine, low, high, ahead, behind, *early, left_interface, right_interface))
 
 
 def combine_kernel(got, out, alpha_ref, *, scale):
@@ -209,6 +297,7 @@
         ),
         in_specs=[vmem],
         out_specs=(vmem, vmem),
+        compiler_params=pltpu.CompilerParams(vmem_limit_bytes=ROOM),
         name="combine_part",
     )(*near(got))
 
@@ -258,14 +347,10 @@
         inverse[first:last, :] = right
         if last < W:
             done = jnp.concatenate([left, right], axis=1)
-            change = lax.dot_general(
-                left,
-                done,
-                (((0,), (0,)), ((), ())),
-                precision=highest,
-                preferred_element_type=jnp.float32,
-            )
-            table[last:, :] = table[last:, :] - change[last:, :]
+            turned = left.T
+            for low, high in ((last, last + SIZE), (last + SIZE, W)):
+                if low < high:
+                    table[low:high, :] = table[low:high, :] - product(turned[low:high], done)
 
     alpha = alpha_ref[0:1, :]
     core = [
@@ -301,6 +386,7 @@
         in_specs=[vmem] * 4,
         out_specs=(vmem,) * 3,
         scratch_shapes=[pltpu.VMEM((W, 2 * W), jnp.float32)],
+        compiler_params=pltpu.CompilerParams(vmem_limit_bytes=ROOM),
         name="factor_part",
     )(*near(whole, alpha, mine, owned))
     interface = pl.pallas_call(
@@ -308,6 +394,7 @@
         out_shape=jax.ShapeDtypeStruct((3, piece, W), jnp.float32),
         in_specs=[pl.BlockSpec(memory_space=pltpu.SMEM), vmem, vmem],
         out_specs=vmem,
+        compiler_params=pltpu.CompilerParams(vmem_limit_bytes=ROOM),
         name="interface_part",
     )(rank, *near(whole, inverse))
     return basis, triangle, interface
@@ -340,7 +427,10 @@
     ahead, behind = parcel(3, 1), parcel(2, 0)
     low = lax.ppermute(ahead, ("x", "y", "core", "rank"), forward)
     high = lax.ppermute(behind, ("x", "y", "core", "rank"), backward)
-    blocks, owned = local_part(mine, low, high, ahead, behind, left_interface, right_interface)
+    early = early_part(mine, ahead, behind, left_interface, right_interface)
+    blocks, owned = local_part(
+        mine, low, high, ahead, behind, early, left_interface, right_interface
+    )
 
     block = jnp.sum(exchange(blocks.reshape(8, 192, width), ("x", "core")), axis=0)
     block = block.reshape(8, 3, 8, width)

time: 129 us -> 126 us (0.977)
  Pallas kernels: 15.7 us -> 13.8 us
    pallas_call x1, Pallas kernels: 7.72 us -> 5.88 us  [local_part(): pl.pallas_call(local_kernel, out_shape=(pltpu.VMEM((HALF * 24, W), jnp.fl...]
  transfers between devices with their start and end apart: 4 -> 4, of which waited for: 4 -> 4; matrix products, arithmetic and copies ran while one was open for 0% -> 0% of each run, Pallas kernels for 1% -> 2%
where the time goes in v4:
time: 126 us
  blocking collectives  67.3 us (53%)
  waiting for transfers between devices  21.1 us (17%)
  starting transfers between devices  19.6 us (16%)
  Pallas kernels  13.8 us (11%)
  other arithmetic  1.92 us (2%)
    all_to_all x4, blocking collectives, exchange(): return lax.all_to_all(blocks, axis, 0, 0, tiled=True)  67.3 us
    all_to_all x2, waiting for transfers between devices, exchange(): return lax.all_to_all(blocks, axis, 0, 0, tiled=True)  16.7 us
    all_to_all x2, starting transfers between devices, exchange(): return lax.all_to_all(blocks, axis, 0, 0, tiled=True)  14.4 us
    pallas_call x1, Pallas kernels, local_part(): pl.pallas_call(local_kernel, out_shape=(pltpu.VMEM((HALF * 24, W), jnp.fl...  5.88 us
    pallas_call x1, Pallas kernels, final_part(): pl.pallas_call(factor_kernel, out_shape=(pltpu.VMEM((ranks, 2, piece, W),...  5.74 us
    ppermute x1, waiting for transfers between devices, shards(): low = lax.ppermute(ahead, ('x', 'y', 'core', 'rank'), forward)  4.1 us
    ppermute x1, starting transfers between devices, shards(): low = lax.ppermute(ahead, ('x', 'y', 'core', 'rank'), forward)  2.97 us
  transfers between devices with their start and end apart: 4, of which 4 were waited for; matrix products, arithmetic and copies ran while one was open for 0% of the time, Pallas kernels for 2%

profile of v4, /device:TPU:1, one launch (start us, length us, event | category | flops | bytes accessed | tf_op | source)
XLA Modules:
  0.0 125.7 jit_solution(17050383665373544225)
XLA Ops:
  0.6 1.7 %pad_maximum_fusion = f32[8,4,16,128]{3,2,1,0:T(8,128)} fusion(f32[8,2,16,128]{3,2,1,0:T(8,128)} %bitcast.37, f32[8,2,16,128]{3,2,1,0:T(8,128)} %bitcast.38), kind=kLoop, calls=%fused_computation | loop fusion | flops 65536 | bytes 524288 | tf_op jit(solution)/shard_map/concatenate | solution.py:415
  2.3 0.0 copy-start.2
  2.3 11.0 %all-to-all-start = ((f32[8,4,16,128]{3,2,1,0:T(8,128)}), f32[8,4,16,128]{3,2,1,0:T(8,128)S(1)}, u32[]{:S(2)}, u32[]{:S(2)}) async-start(f32[8,4,16,128]{3,2,1,0:T(8,128)} %pad_maximum_fusion), calls=%async_computation | async-start | bytes 524288 | tf_op jit(solution)/shard_map/all_to_all | solution.py:17
  13.3 0.0 copy-done.2
  13.3 0.1 constant_dynamic-slice_fusion
  13.4 0.2 slice_reduce_fusion
  13.6 10.2 %all-to-all-done.mine = f32[8,4,16,128]{3,2,1,0:T(8,128)S(1)} async-done(((f32[8,4,16,128]{3,2,1,0:T(8,128)}), f32[8,4,16,128]{3,2,1,0:T(8,128)S(1)}, u32[]{:S(2)}, u32[]{:S(2)}) %all-to-all-start) | async-done | bytes 262176 | tf_op jit(solution)/shard_map/all_to_all | solution.py:17
  23.8 0.0 copy-start
  23.8 0.0 copy-start.1
  23.9 0.2 fusion.1
  24.0 2.3 %collective-permute-start.1 = (f32[416,128]{1,0:T(8,128)S(1)}, f32[416,128]{1,0:T(8,128)S(1)}, u32[]{:S(2)}, u32[]{:S(2)}) collective-permute-start(f32[416,128]{1,0:T(8,128)S(1)} %get-tuple-element.29.behind), channel_id=1, source_target_pairs={{1,0},{2,1},{3,2},{4,3},{5,4},{6,5},{7,6},{8,7},{9,8},{10,9},{11,1... | collective-permute-start | bytes 638984 | tf_op jit(solution)/shard_map/ppermute | solution.py:429
  26.3 3.0 %collective-permute-start = (f32[416,128]{1,0:T(8,128)S(1)}, f32[416,128]{1,0:T(8,128)S(1)}, u32[]{:S(2)}, u32[]{:S(2)}) collective-permute-start(f32[416,128]{1,0:T(8,128)S(1)} %get-tuple-element.30.ahead), channel_id=1, source_target_pairs={{0,1},{1,2},{2,3},{3,4},{4,5},{5,6},{6,7},{7,8},{8,9},{9,10},{10,1... | collective-permute-start | bytes 638984 | tf_op jit(solution)/shard_map/ppermute | solution.py:428
  29.3 0.0 copy-done
  29.3 0.0 copy-done.1
  29.3 0.9 early_part.1
  30.3 0.3 collective-permute-done.1.high
  30.6 4.1 %collective-permute-done.low = f32[416,128]{1,0:T(8,128)S(1)} collective-permute-done((f32[416,128]{1,0:T(8,128)S(1)}, f32[416,128]{1,0:T(8,128)S(1)}, u32[]{:S(2)}, u32[]{:S(2)}) %collective-permute-start) | collective-permute-done | bytes 213024 | tf_op jit(solution)/shard_map/ppermute | solution.py:428
  34.7 5.9 %local_part.1 = (f32[1536,128]{1,0:T(8,128)S(1)}, f32[256,128]{1,0:T(8,128)S(1)}) custom-call(f32[8,4,16,128]{3,2,1,0:T(8,128)S(1)} %all-to-all-done.mine, f32[416,128]{1,0:T(8,128)S(1)} %collective-permute-done.low, f32[416,128]{1,0:T(8,128)S(1)} %collective-permute-done.1.high, f32[416,128]{1,0:T(8,128)S(1)} %get-tuple-element.30.ahead, ...), custom_call_target="tpu_custom_call" | custom-call | tf_op jit(solution)/shard_map/local_part/pallas_call | solution.py:254
  40.6 21.2 %all_to_all.30 = f32[8,192,128]{2,1,0:T(8,128)S(1)} all-to-all(f32[8,192,128]{2,1,0:T(8,128)S(1)} %bitcast.26), channel_id=1, replica_groups=mesh['x'=4,'y'=8,'core'=2,'rank'=8] {'x','core'}, dimensions={0} | all-to-all | bytes 1572864 | tf_op jit(solution)/shard_map/all_to_all | solution.py:17
  61.9 0.1 copy.13
  62.0 19.1 %all_to_all.31 = f32[64,4,128]{2,1,0:T(4,128)S(1)} all-to-all(f32[64,4,128]{2,1,0:T(4,128)S(1)} %copy.13), channel_id=1, replica_groups=mesh['x'=4,'y'=8,'core'=2,'rank'=8] {'y','rank'}, dimensions={0} | all-to-all | bytes 262144 | tf_op jit(solution)/shard_map/all_to_all | solution.py:17
  81.0 0.1 combine_part.1
  81.1 14.6 %all_to_all.32 = f32[64,1,128]{2,1,0:T(1,128)S(1)} all-to-all(f32[64,1,128]{2,1,0:T(1,128)S(1)} %bitcast.28), channel_id=1, replica_groups=mesh['x'=4,'y'=8,'core'=2,'rank'=8] {'y','rank'}, dimensions={0} | all-to-all | bytes 65536 | tf_op jit(solution)/shard_map/all_to_all | solution.py:17
  95.8 12.4 %all_to_all.33 = f32[8,64,128]{2,1,0:T(8,128)S(1)} all-to-all(f32[8,64,128]{2,1,0:T(8,128)S(1)} %broadcast_in_dim.19), channel_id=1, replica_groups=mesh['x'=4,'y'=8,'core'=2,'rank'=8] {'x','core'}, dimensions={0} | all-to-all | bytes 524288 | tf_op jit(solution)/shard_map/all_to_all | solution.py:17
  108.2 5.7 %factor_part.1 = (f32[8,2,16,128]{3,2,1,0:T(8,128)}, f32[128,128]{1,0:T(8,128)}, f32[128,128]{1,0:T(8,128)S(1)}) custom-call(f32[512,128]{1,0:T(8,128)S(1)} %bitcast.24, f32[8,128]{1,0:T(8,128)S(1)} %get-tuple-element.18.alpha_ref, f32[8,4,16,128]{3,2,1,0:T(8,128)S(1)} %all-to-all-done.mine, f32[256,128]{1,0:T(8,128)S(1)} %get-tuple-element.19.owned), custom_call_target="tpu_custom_call" | custom-call | tf_op jit(solution)/shard_map/factor_part/pallas_call | solution.py:379
  114.0 3.4 %all-to-all-start.5 = ((f32[8,2,16,128]{3,2,1,0:T(8,128)}), f32[8,2,16,128]{3,2,1,0:T(8,128)S(1)}, u32[]{:S(2)}, u32[]{:S(2)}) async-start(f32[8,2,16,128]{3,2,1,0:T(8,128)} %get-tuple-element.20), calls=%async_computation.5 | async-start | bytes 262144 | tf_op jit(solution)/shard_map/all_to_all | solution.py:17
  117.4 1.2 interface_part.1
  118.5 6.5 %all-to-all-done.5 = f32[8,2,16,128]{3,2,1,0:T(8,128)S(1)} async-done(((f32[8,2,16,128]{3,2,1,0:T(8,128)}), f32[8,2,16,128]{3,2,1,0:T(8,128)S(1)}, u32[]{:S(2)}, u32[]{:S(2)}) %all-to-all-start.5) | async-done | bytes 131104 | tf_op jit(solution)/shard_map/all_to_all | solution.py:17
  125.0 0.7 copy.17
  (10 shorter events, 0.1 us)
Async XLA Ops:
  2.3 11.0 %copy-start.2 = (f32[3,3,3,16]{3,2,1,0:T(4,128)S(1)}, f32[3,3,3,16]{3,2,1,0:T(4,128)}, u32[]{:S(2)}) copy-start(f32[3,3,3,16]{3,2,1,0:T(4,128)} %param.9) | copy-start | bytes 5188
  2.3 21.5 %all-to-all-start = ((f32[8,4,16,128]{3,2,1,0:T(8,128)}), f32[8,4,16,128]{3,2,1,0:T(8,128)S(1)}, u32[]{:S(2)}, u32[]{:S(2)}) async-start(f32[8,4,16,128]{3,2,1,0:T(8,128)} %pad_maximum_fusion), calls=%async_computation | async-start | bytes 524288 | tf_op jit(solution)/shard_map/all_to_all | solution.py:17
  23.8 5.5 %copy-start = (f32[3,128,128]{2,1,0:T(8,128)S(1)}, f32[3,128,128]{2,1,0:T(8,128)}, u32[]{:S(2)}) copy-start(f32[3,128,128]{2,1,0:T(8,128)} %left_ref.3) | copy-start | bytes 589828
  23.8 5.5 %copy-start.1 = (f32[3,128,128]{2,1,0:T(8,128)S(1)}, f32[3,128,128]{2,1,0:T(8,128)}, u32[]{:S(2)}) copy-start(f32[3,128,128]{2,1,0:T(8,128)} %right_ref.3) | copy-start | bytes 589828
  24.0 6.6 %collective-permute-start.1 = (f32[416,128]{1,0:T(8,128)S(1)}, f32[416,128]{1,0:T(8,128)S(1)}, u32[]{:S(2)}, u32[]{:S(2)}) collective-permute-start(f32[416,128]{1,0:T(8,128)S(1)} %get-tuple-element.29.behind), channel_id=1, source_target_pairs={{1,0},{2,1},{3,2},{4,3},{5,4},{6,5},{7,6},{8,7},{9,8},{10,9},{11,1... | collective-permute-start | bytes 638984 | tf_op jit(solution)/shard_map/ppermute | solution.py:429
  26.3 8.4 %collective-permute-start = (f32[416,128]{1,0:T(8,128)S(1)}, f32[416,128]{1,0:T(8,128)S(1)}, u32[]{:S(2)}, u32[]{:S(2)}) collective-permute-start(f32[416,128]{1,0:T(8,128)S(1)} %get-tuple-element.30.ahead), channel_id=1, source_target_pairs={{0,1},{1,2},{2,3},{3,4},{4,5},{5,6},{6,7},{7,8},{8,9},{9,10},{10,1... | collective-permute-start | bytes 638984 | tf_op jit(solution)/shard_map/ppermute | solution.py:428
  114.0 11.0 %all-to-all-start.5 = ((f32[8,2,16,128]{3,2,1,0:T(8,128)}), f32[8,2,16,128]{3,2,1,0:T(8,128)S(1)}, u32[]{:S(2)}, u32[]{:S(2)}) async-start(f32[8,2,16,128]{3,2,1,0:T(8,128)} %get-tuple-element.20), calls=%async_computation.5 | async-start | bytes 262144 | tf_op jit(solution)/shard_map/all_to_all | solution.py:17

commit v5 on v4

--- a/solution.py
+++ b/solution.py
@@ -53,6 +53,36 @@
     return [pltpu.with_memory_space_constraint(value, pltpu.VMEM) for value in values]
 
 
+def pack_kernel(start, right, packed, done):
+    copies = []
+    for field, ref in enumerate((start, right)):
+        for half in range(2):
+            part = pl.ds(half * (ref.shape[0] // 2), ref.shape[0] // 2)
+            copies.append(
+                pltpu.make_async_copy(
+                    ref.at[part], packed.at[part, pl.ds(2 * field, 2)], done.at[2 * field + half]
+                )
+            )
+    for copy in copies:
+        copy.start()
+    for copy in copies:
+        copy.wait()
+
+
+def pack_part(start, right):
+    anywhere = pl.BlockSpec(memory_space=pltpu.HBM)
+    ranks, _, piece, _ = start.shape
+    return pl.pallas_call(
+        pack_kernel,
+        out_shape=jax.ShapeDtypeStruct((ranks, 4, piece, W), jnp.float32),
+        in_specs=[anywhere] * 2,
+        out_specs=anywhere,
+        scratch_shapes=[pltpu.SemaphoreType.DMA((4,))],
+        compiler_params=pltpu.CompilerParams(vmem_limit_bytes=ROOM),
+        name="pack_part",
+    )(*(pltpu.with_memory_space_constraint(value, pltpu.HBM) for value in (start, right)))
+
+
 def own_slot(mine, index):
     return mine[:, index].reshape(W, W)
 
@@ -65,12 +95,9 @@
 
 
 def couple(place, sources, target, base, left_first):
-    ref, start = place
     used = {offset for offset, _ in sources}
     weight = {
-        (i, j, offset): jnp.broadcast_to(
-            ref[start + i * 9 + j * 3 + offset : start + i * 9 + j * 3 + offset + 1, :], (8, W)
-        )
+        (i, j, offset): jnp.broadcast_to(place(i, j, offset), (8, W))
         for i in range(3)
         for j in range(3)
         for offset in used
@@ -121,36 +148,74 @@
     return load, store
 
 
-def early_kernel(mine, ahead, behind, left_ref, right_ref, terms, partial, shifted, mixed):
+def own_row(table, mode):
+    def row(i, j, offset):
+        at = 32 * mode + 9 * i + 3 * j + offset
+        return table[at : at + 1, :]
+
+    return row
+
+
+def sent_row(parcel):
+    return lambda i, j, offset: parcel[2 * W + 3 * i + j : 2 * W + 3 * i + j + 1, :]
+
+
+def parcel_kernel(mine, table, left_ref, right_ref, ahead, behind, terms, coupled):
     right_rows = halves(right_ref[...].reshape(3 * W, W))
+    left_lanes = halves(jnp.concatenate([left_ref[0], left_ref[1], left_ref[2]], axis=1))
+    contract(right_rows, [own_slot(mine, 0), own_slot(mine, 1)], terms, 0)
+    for i in range(2):
+        present = [(1 - i + k, term_rows(terms, k)) for k in range(2)]
+        couple(own_row(table, i), present, lanes_of(coupled, i)[1], None, False)
+    applied = split_product(halves(coupled[...].reshape(2 * W, 3 * W)), left_lanes, 1)
+    for i, parcel, offset in ((0, behind, 0), (1, ahead, 2)):
+        parcel[0:W] = own_slot(mine, i)
+        parcel[W : 2 * W] = own_slot(mine, 2 + i) - applied[i * W : (i + 1) * W]
+        parcel[2 * W : 2 * W + 16] = jnp.zeros((16, W), jnp.float32)
+        row = own_row(table, i)
+        for alpha in range(3):
+            for beta in range(3):
+                at = 2 * W + 3 * alpha + beta
+                parcel[at : at + 1, :] = row(alpha, beta, offset)
+
+
+def parcel_part(mine, table, left_interface, right_interface):
+    vmem = pl.BlockSpec(memory_space=pltpu.VMEM)
+    return pl.pallas_call(
+        parcel_kernel,
+        out_shape=(
+            pltpu.VMEM((2 * W + 16, W), jnp.float32),
+            pltpu.VMEM((2 * W + 16, W), jnp.float32),
+            pltpu.VMEM((2, 3 * W, W), jnp.float32),
+        ),
+        in_specs=[vmem] * 4,
+        out_specs=(vmem,) * 3,
+        scratch_shapes=[pltpu.VMEM((2, W, 3 * W), jnp.float32)],
+        compiler_params=pltpu.CompilerParams(vmem_limit_bytes=ROOM),
+        name="parcel_part",
+    )(*near(mine, table, left_interface, right_interface))
+
+
+def early_kernel(mine, table, left_ref, shifted, mixed):
     left_rows = halves(left_ref[...].reshape(3 * W, W))
-    fields = [own_slot(mine, 0), own_slot(mine, 1)]
-    weights = [(behind, 3 * W), (ahead, 3 * W)]
-    contract(right_rows, fields, terms, 0)
-    stack = halves(jnp.concatenate(fields, axis=0))
+    stack = halves(jnp.concatenate([own_slot(mine, 0), own_slot(mine, 1)], axis=0))
     mixed[...] = split_product(stack, left_rows, 1).reshape(2, W, 3 * W)
     for i in range(2):
-        present = [(1 - i + k, term_rows(terms, k)) for k in range(2)]
-        couple(weights[i], present, lanes_of(partial, i)[1], None, False)
         present = [(1 - i + k, mixed_rows(mixed, k)) for k in range(2)]
-        couple(weights[i], present, moved_of(shifted, (), i)[1], None, True)
-
-
-def early_part(mine, ahead, behind, left_interface, right_interface):
+        couple(own_row(table, i), present, moved_of(shifted, (), i)[1], None, True)
+
+
+def early_part(mine, table, left_interface):
     vmem = pl.BlockSpec(memory_space=pltpu.VMEM)
     return pl.pallas_call(
         early_kernel,
-        out_shape=(
-            pltpu.VMEM((2, 3 * W, W), jnp.float32),
-            pltpu.VMEM((2, W, 3 * W), jnp.float32),
-            pltpu.VMEM((3 * W, 2 * W), jnp.float32),
-        ),
-        in_specs=[vmem] * 5,
-        out_specs=(vmem,) * 3,
+        out_shape=pltpu.VMEM((3 * W, 2 * W), jnp.float32),
+        in_specs=[vmem] * 3,
+        out_specs=vmem,
         scratch_shapes=[pltpu.VMEM((2, W, 3 * W), jnp.float32)],
         compiler_params=pltpu.CompilerParams(vmem_limit_bytes=ROOM),
         name="early_part",
-    )(*near(mine, ahead, behind, left_interface, right_interface))
+    )(*near(mine, table, left_interface))
 
 
 def local_kernel(
@@ -160,7 +225,7 @@
     ahead,
     behind,
     own_terms,
-    partial,
+    table,
     shifted,
     left_ref,
     right_ref,
@@ -172,29 +237,25 @@
     moved,
     pair,
 ):
-    outer = [low[0:W], low[W : 2 * W], high[0:W], high[W : 2 * W]]
-    sources = [low[2 * W : 3 * W], own_slot(mine, 2), own_slot(mine, 3), high[2 * W : 3 * W]]
-    weights = [(low, 3 * W), (behind, 3 * W), (ahead, 3 * W), (high, 3 * W)]
+    weights = [own_row(table, 0), own_row(table, 1)]
     right_rows = halves(right_ref[...].reshape(3 * W, W))
     left_rows = halves(left_ref[...].reshape(3 * W, W))
     left_lanes = halves(jnp.concatenate([left_ref[0], left_ref[1], left_ref[2]], axis=1))
-    store = lanes_of(coupled, 0)[1]
-
-    def finish():
-        return split_product(halves(coupled[0]), left_lanes, 1)
-
-    contract(right_rows, outer, terms, 0)
-    lists = [
-        [(0, term_rows(terms, 0)), (1, term_rows(terms, 1)), (2, term_rows(own_terms, 0))],
-        [(0, term_rows(terms, 1))],
-        [(2, term_rows(terms, 2))],
-        [(0, term_rows(own_terms, 1)), (1, term_rows(terms, 2)), (2, term_rows(terms, 3))],
+    contract(right_rows, [low[0:W], high[0:W]], terms, 0)
+    places = [
+        (sent_row(low), (2, term_rows(own_terms, 0))),
+        (weights[0], (0, term_rows(terms, 0))),
+        (weights[1], (2, term_rows(terms, 1))),
+        (sent_row(high), (0, term_rows(own_terms, 1))),
     ]
-    residual = []
     for i in range(4):
-        base = lanes_of(partial, i - 1)[0] if i in (1, 2) else None
-        couple(weights[i], lists[i], store, base, False)
-        residual.append(sources[i] - finish())
+        couple(places[i][0], [places[i][1]], lanes_of(coupled, i)[1], None, False)
+    applied = split_product(halves(coupled[...].reshape(4 * W, 3 * W)), left_lanes, 1)
+    residual = [
+        source[W : 2 * W] - applied[i * W : (i + 1) * W]
+        for i, source in enumerate((low, behind, ahead, high))
+    ]
+    outer = [None, low[0:W], high[0:W]]
     pair[0], pair[3] = outer[1], outer[2]
     pair[1], pair[2] = own_slot(mine, 0), own_slot(mine, 1)
     for i in range(4):
@@ -206,8 +267,10 @@
     energy = jnp.zeros((1, 1), jnp.float32)
     for i in range(2):
         present = [(offset, term_rows(terms, i + offset)) for offset in range(3)]
-        couple(weights[1 + i], present, store, None, False)
-        image = finish()
+        couple(weights[i], present, lanes_of(coupled, i)[1], None, False)
+    images = split_product(halves(coupled[0:2].reshape(2 * W, 3 * W)), left_lanes, 1)
+    for i in range(2):
+        image = images[i * W : (i + 1) * W]
         along = along + jnp.sum(pair[5 + i] * image, keepdims=True)
         energy = energy + jnp.sum(image * image, keepdims=True)
 
@@ -216,9 +279,9 @@
     for i in range(2):
         base = moved_of(shifted, (), i)[0]
         present = [(2 * i, mixed_rows(mixed, i))]
-        couple(weights[1 + i], present, moved_of(moved, (0,), i)[1], base, True)
+        couple(weights[i], present, moved_of(moved, (0,), i)[1], base, True)
         present = [(offset, mixed_rows(mixed, 2 + i + offset)) for offset in range(3)]
-        couple(weights[1 + i], present, moved_of(moved, (1,), i)[1], None, True)
+        couple(weights[i], present, moved_of(moved, (1,), i)[1], None, True)
 
     both = jnp.concatenate(
         [
@@ -249,7 +312,7 @@
         blocks[pl.ds(8 * version + 7, HALF, stride=24), :] = extra
 
 
-def local_part(mine, low, high, ahead, behind, early, left_interface, right_interface):
+def local_part(mine, low, high, ahead, behind, terms, table, shifted, left_interface, right_interface):
     vmem = pl.BlockSpec(memory_space=pltpu.VMEM)
     return pl.pallas_call(
         local_kernel,
@@ -262,13 +325,26 @@
         scratch_shapes=[
             pltpu.VMEM((4, 3 * W, W), jnp.float32),
             pltpu.VMEM((6, W, 3 * W), jnp.float32),
-            pltpu.VMEM((1, W, 3 * W), jnp.float32),
+            pltpu.VMEM((4, W, 3 * W), jnp.float32),
             pltpu.VMEM((2, 3 * W, 2 * W), jnp.float32),
             pltpu.VMEM((8, W, W), jnp.float32),
         ],
         compiler_params=pltpu.CompilerParams(vmem_limit_bytes=ROOM),
         name="local_part",
-    )(*near(mine, low, high, ahead, behind, *early, left_interface, right_interface))
+    )(
+        *near(
+            mine,
+            low,
+            high,
+            ahead,
+            behind,
+            terms,
+            table,
+            shifted,
+            left_interface,
+            right_interface,
+        )
+    )
 
 
 def combine_kernel(got, out, alpha_ref, *, scale):
@@ -412,7 +488,7 @@
 
     start = start_core.reshape(ranks, own, piece, width)
     right = right_side.reshape(ranks, own, piece, width)
-    mine = exchange(jnp.concatenate([start, right], axis=1), "rank")
+    mine = exchange(pack_part(start, right), "rank")
 
     table = lax.dynamic_slice_in_dim(couplings.reshape(27, height), rank_index * own, own, 1)
     table = jnp.pad(table, ((0, 5), (0, 0))).T[:, :, None]
@@ -420,16 +496,12 @@
     forward = [(i, i + 1) for i in range(count - 1)]
     backward = [(target, source) for source, target in forward]
 
-    def parcel(source, column):
-        parts = [mine[:, slot].reshape(width, width) for slot in (0, 1, source)]
-        return jnp.concatenate(parts + [table[32 * column : 32 * column + 32]], axis=0)
-
-    ahead, behind = parcel(3, 1), parcel(2, 0)
+    ahead, behind, terms = parcel_part(mine, table, left_interface, right_interface)
     low = lax.ppermute(ahead, ("x", "y", "core", "rank"), forward)
     high = lax.ppermute(behind, ("x", "y", "core", "rank"), backward)
-    early = early_part(mine, ahead, behind, left_interface, right_interface)
+    shifted = early_part(mine, table, left_interface)
     blocks, owned = local_part(
-        mine, low, high, ahead, behind, early, left_interface, right_interface
+        mine, low, high, ahead, behind, terms, table, shifted, left_interface, right_interface
     )
 
     block = jnp.sum(exchange(blocks.reshape(8, 192, width), ("x", "core")), axis=0)

time: 126 us -> 134 us (1.063)
  Pallas kernels: 13.8 us -> 22.6 us
  waiting for transfers between devices: 21.1 us -> 18.1 us
  blocking collectives: 67.3 us -> 70 us
  other arithmetic: 1.92 us -> 0.05 us
  starting transfers between devices: 19.6 us -> 21.1 us
    pallas_call x1 -> x3, Pallas kernels: 0.94 us -> 10.8 us  [the longest x1 9.08 us: pack_part(): pl.pallas_call(pack_kernel, out_shape=jax.ShapeDtypeStruct((ranks, 4, pie...]
    ppermute x1, waiting for transfers between devices: 4.1 us -> 0.23 us  [shards(): low = lax.ppermute(ahead, ('x', 'y', 'core', 'rank'), forward)]
    all_to_all x4, blocking collectives: 67.3 us -> 70 us  [exchange(): return lax.all_to_all(blocks, axis, 0, 0, tiled=True)]
    ppermute x1, starting transfers between devices: 2.31 us -> 4.85 us  [shards(): high = lax.ppermute(behind, ('x', 'y', 'core', 'rank'), backward)]
    concatenate x2 -> x0, other arithmetic: 1.87 us -> none  [the longest x1 1.69 us: shards(): mine = exchange(jnp.concatenate([start, right], axis=1), 'rank')]
  transfers between devices with their start and end apart: 4 -> 4, of which waited for: 4 -> 4; matrix products, arithmetic and copies ran while one was open for 0% -> 0% of each run, Pallas kernels for 2% -> 1%
where the time goes in v5:
time: 134 us
  blocking collectives  70 us (52%)
  Pallas kernels  22.6 us (17%)
  starting transfers between devices  21.1 us (16%)
  waiting for transfers between devices  18.1 us (14%)
    all_to_all x4, blocking collectives, exchange(): return lax.all_to_all(blocks, axis, 0, 0, tiled=True)  70 us
    all_to_all x2, waiting for transfers between devices, exchange(): return lax.all_to_all(blocks, axis, 0, 0, tiled=True)  16.7 us
    all_to_all x2, starting transfers between devices, exchange(): return lax.all_to_all(blocks, axis, 0, 0, tiled=True)  14.4 us
    pallas_call x1, Pallas kernels, pack_part(): pl.pallas_call(pack_kernel, out_shape=jax.ShapeDtypeStruct((ranks, 4, pie...  9.08 us
    pallas_call x1, Pallas kernels, final_part(): pl.pallas_call(factor_kernel, out_shape=(pltpu.VMEM((ranks, 2, piece, W),...  5.74 us
    ppermute x1, starting transfers between devices, shards(): high = lax.ppermute(behind, ('x', 'y', 'core', 'rank'), backward)  4.85 us
    pallas_call x1, Pallas kernels, local_part(): pl.pallas_call(local_kernel, out_shape=(pltpu.VMEM((HALF * 24, W), jnp.fl...  4.82 us
  transfers between devices with their start and end apart: 4, of which 4 were waited for; matrix products, arithmetic and copies ran while one was open for 0% of the time, Pallas kernels for 1%

profile of v5, /device:TPU:1, one launch (start us, length us, event | category | flops | bytes accessed | tf_op | source)
XLA Modules:
  0.0 133.8 jit_solution(7100960659668510600)
XLA Ops:
  0.6 9.1 %pack_part.1 = f32[8,4,16,128]{3,2,1,0:T(8,128)} custom-call(f32[8,2,16,128]{3,2,1,0:T(8,128)} %bitcast.29, f32[8,2,16,128]{3,2,1,0:T(8,128)} %bitcast.30), custom_call_target="tpu_custom_call" | custom-call | tf_op jit(solution)/shard_map/pack_part/pallas_call | solution.py:75
  9.7 0.0 copy-start.2
  9.7 0.0 copy-start
  9.7 0.0 copy-start.1
  9.8 11.0 %all-to-all-start = ((f32[8,4,16,128]{3,2,1,0:T(8,128)}), f32[8,4,16,128]{3,2,1,0:T(8,128)S(1)}, u32[]{:S(2)}, u32[]{:S(2)}) async-start(f32[8,4,16,128]{3,2,1,0:T(8,128)} %pack_part.1), calls=%async_computation | async-start | bytes 524288 | tf_op jit(solution)/shard_map/all_to_all | solution.py:17
  20.8 0.0 copy-done.2
  20.8 0.1 constant_dynamic-slice_fusion
  20.9 0.1 copy.14
  20.9 0.1 broadcast_in_dim.21
  21.0 10.2 %all-to-all-done.mine = f32[8,4,16,128]{3,2,1,0:T(8,128)S(1)} async-done(((f32[8,4,16,128]{3,2,1,0:T(8,128)}), f32[8,4,16,128]{3,2,1,0:T(8,128)S(1)}, u32[]{:S(2)}, u32[]{:S(2)}) %all-to-all-start) | async-done | bytes 262176 | tf_op jit(solution)/shard_map/all_to_all | solution.py:17
  31.2 0.1 broadcast_in_dim.22.table
  31.3 0.0 copy-done
  31.3 0.0 copy-done.1
  31.3 1.2 parcel_part.1
  32.5 1.9 %collective-permute-start = (f32[272,128]{1,0:T(8,128)S(1)}, f32[272,128]{1,0:T(8,128)S(1)}, u32[]{:S(2)}, u32[]{:S(2)}) collective-permute-start(f32[272,128]{1,0:T(8,128)S(1)} %get-tuple-element.13.ahead), channel_id=1, source_target_pairs={{0,1},{1,2},{2,3},{3,4},{4,5},{5,6},{6,7},{7,8},{8,9},{9,10},{10,1... | collective-permute-start | bytes 417800 | tf_op jit(solution)/shard_map/ppermute | solution.py:500
  34.4 4.9 %collective-permute-start.1 = (f32[272,128]{1,0:T(8,128)S(1)}, f32[272,128]{1,0:T(8,128)S(1)}, u32[]{:S(2)}, u32[]{:S(2)}) collective-permute-start(f32[272,128]{1,0:T(8,128)S(1)} %get-tuple-element.14.behind), channel_id=1, source_target_pairs={{1,0},{2,1},{3,2},{4,3},{5,4},{6,5},{7,6},{8,7},{9,8},{10,9},{11,1... | collective-permute-start | bytes 417800 | tf_op jit(solution)/shard_map/ppermute | solution.py:501
  39.3 0.6 early_part.1.shifted
  39.8 0.2 collective-permute-done.low
  40.1 1.2 collective-permute-done.1.high
  41.3 4.8 %local_part.1 = (f32[1536,128]{1,0:T(8,128)S(1)}, f32[256,128]{1,0:T(8,128)S(1)}) custom-call(f32[8,4,16,128]{3,2,1,0:T(8,128)S(1)} %all-to-all-done.mine, f32[272,128]{1,0:T(8,128)S(1)} %collective-permute-done.low, f32[272,128]{1,0:T(8,128)S(1)} %collective-permute-done.1.high, f32[272,128]{1,0:T(8,128)S(1)} %get-tuple-element.13.ahead, ...), custom_call_target="tpu_custom_call" | custom-call | tf_op jit(solution)/shard_map/local_part/pallas_call | solution.py:317
  46.1 22.1 %all_to_all.30 = f32[8,192,128]{2,1,0:T(8,128)S(1)} all-to-all(f32[8,192,128]{2,1,0:T(8,128)S(1)} %bitcast.22), channel_id=1, replica_groups=mesh['x'=4,'y'=8,'core'=2,'rank'=8] {'x','core'}, dimensions={0} | all-to-all | bytes 1572864 | tf_op jit(solution)/shard_map/all_to_all | solution.py:17
  68.3 0.1 copy.16
  68.4 20.8 %all_to_all.31 = f32[64,4,128]{2,1,0:T(4,128)S(1)} all-to-all(f32[64,4,128]{2,1,0:T(4,128)S(1)} %copy.16), channel_id=1, replica_groups=mesh['x'=4,'y'=8,'core'=2,'rank'=8] {'y','rank'}, dimensions={0} | all-to-all | bytes 262144 | tf_op jit(solution)/shard_map/all_to_all | solution.py:17
  89.2 0.1 combine_part.1
  89.3 14.6 %all_to_all.32 = f32[64,1,128]{2,1,0:T(1,128)S(1)} all-to-all(f32[64,1,128]{2,1,0:T(1,128)S(1)} %bitcast.24), channel_id=1, replica_groups=mesh['x'=4,'y'=8,'core'=2,'rank'=8] {'y','rank'}, dimensions={0} | all-to-all | bytes 65536 | tf_op jit(solution)/shard_map/all_to_all | solution.py:17
  104.0 12.4 %all_to_all.33 = f32[8,64,128]{2,1,0:T(8,128)S(1)} all-to-all(f32[8,64,128]{2,1,0:T(8,128)S(1)} %broadcast_in_dim.25), channel_id=1, replica_groups=mesh['x'=4,'y'=8,'core'=2,'rank'=8] {'x','core'}, dimensions={0} | all-to-all | bytes 524288 | tf_op jit(solution)/shard_map/all_to_all | solution.py:17
  116.4 5.7 %factor_part.1 = (f32[8,2,16,128]{3,2,1,0:T(8,128)}, f32[128,128]{1,0:T(8,128)}, f32[128,128]{1,0:T(8,128)S(1)}) custom-call(f32[512,128]{1,0:T(8,128)S(1)} %bitcast.20, f32[8,128]{1,0:T(8,128)S(1)} %get-tuple-element.18.alpha_ref, f32[8,4,16,128]{3,2,1,0:T(8,128)S(1)} %all-to-all-done.mine, f32[256,128]{1,0:T(8,128)S(1)} %get-tuple-element.19.owned), custom_call_target="tpu_custom_call" | custom-call | tf_op jit(solution)/shard_map/factor_part/pallas_call | solution.py:455
  122.1 3.4 %all-to-all-start.5 = ((f32[8,2,16,128]{3,2,1,0:T(8,128)}), f32[8,2,16,128]{3,2,1,0:T(8,128)S(1)}, u32[]{:S(2)}, u32[]{:S(2)}) async-start(f32[8,2,16,128]{3,2,1,0:T(8,128)} %get-tuple-element.20), calls=%async_computation.5 | async-start | bytes 262144 | tf_op jit(solution)/shard_map/all_to_all | solution.py:17
  125.5 1.2 interface_part.1
  126.7 6.5 %all-to-all-done.5 = f32[8,2,16,128]{3,2,1,0:T(8,128)S(1)} async-done(((f32[8,2,16,128]{3,2,1,0:T(8,128)}), f32[8,2,16,128]{3,2,1,0:T(8,128)S(1)}, u32[]{:S(2)}, u32[]{:S(2)}) %all-to-all-start.5) | async-done | bytes 131104 | tf_op jit(solution)/shard_map/all_to_all | solution.py:17
  133.2 0.7 copy.20
  (7 shorter events, 0.1 us)
Async XLA Ops:
  9.7 11.0 %copy-start.2 = (f32[3,3,3,16]{3,2,1,0:T(4,128)S(1)}, f32[3,3,3,16]{3,2,1,0:T(4,128)}, u32[]{:S(2)}) copy-start(f32[3,3,3,16]{3,2,1,0:T(4,128)} %param.9) | copy-start | bytes 5188
  9.7 21.6 %copy-start = (f32[3,128,128]{2,1,0:T(8,128)S(1)}, f32[3,128,128]{2,1,0:T(8,128)}, u32[]{:S(2)}) copy-start(f32[3,128,128]{2,1,0:T(8,128)} %left_ref.5) | copy-start | bytes 589828
  9.7 21.6 %copy-start.1 = (f32[3,128,128]{2,1,0:T(8,128)S(1)}, f32[3,128,128]{2,1,0:T(8,128)}, u32[]{:S(2)}) copy-start(f32[3,128,128]{2,1,0:T(8,128)} %right_ref.3) | copy-start | bytes 589828
  9.8 21.5 %all-to-all-start = ((f32[8,4,16,128]{3,2,1,0:T(8,128)}), f32[8,4,16,128]{3,2,1,0:T(8,128)S(1)}, u32[]{:S(2)}, u32[]{:S(2)}) async-start(f32[8,4,16,128]{3,2,1,0:T(8,128)} %pack_part.1), calls=%async_computation | async-start | bytes 524288 | tf_op jit(solution)/shard_map/all_to_all | solution.py:17
  32.5 7.6 %collective-permute-start = (f32[272,128]{1,0:T(8,128)S(1)}, f32[272,128]{1,0:T(8,128)S(1)}, u32[]{:S(2)}, u32[]{:S(2)}) collective-permute-start(f32[272,128]{1,0:T(8,128)S(1)} %get-tuple-element.13.ahead), channel_id=1, source_target_pairs={{0,1},{1,2},{2,3},{3,4},{4,5},{5,6},{6,7},{7,8},{8,9},{9,10},{10,1... | collective-permute-start | bytes 417800 | tf_op jit(solution)/shard_map/ppermute | solution.py:500
  34.4 6.9 %collective-permute-start.1 = (f32[272,128]{1,0:T(8,128)S(1)}, f32[272,128]{1,0:T(8,128)S(1)}, u32[]{:S(2)}, u32[]{:S(2)}) collective-permute-start(f32[272,128]{1,0:T(8,128)S(1)} %get-tuple-element.14.behind), channel_id=1, source_target_pairs={{1,0},{2,1},{3,2},{4,3},{5,4},{6,5},{7,6},{8,7},{9,8},{10,9},{11,1... | collective-permute-start | bytes 417800 | tf_op jit(solution)/shard_map/ppermute | solution.py:501
  122.1 11.0 %all-to-all-start.5 = ((f32[8,2,16,128]{3,2,1,0:T(8,128)}), f32[8,2,16,128]{3,2,1,0:T(8,128)S(1)}, u32[]{:S(2)}, u32[]{:S(2)}) async-start(f32[8,2,16,128]{3,2,1,0:T(8,128)} %get-tuple-element.20), calls=%async_computation.5 | async-start | bytes 262144 | tf_op jit(solution)/shard_map/all_to_all | solution.py:17

commit v6 on v5

--- a/solution.py
+++ b/solution.py
@@ -51,36 +51,6 @@
 
 def near(*values):
     return [pltpu.with_memory_space_constraint(value, pltpu.VMEM) for value in values]
-
-
-def pack_kernel(start, right, packed, done):
-    copies = []
-    for field, ref in enumerate((start, right)):
-        for half in range(2):
-            part = pl.ds(half * (ref.shape[0] // 2), ref.shape[0] // 2)
-            copies.append(
-                pltpu.make_async_copy(
-                    ref.at[part], packed.at[part, pl.ds(2 * field, 2)], done.at[2 * field + half]
-                )
-            )
-    for copy in copies:
-        copy.start()
-    for copy in copies:
-        copy.wait()
-
-
-def pack_part(start, right):
-    anywhere = pl.BlockSpec(memory_space=pltpu.HBM)
-    ranks, _, piece, _ = start.shape
-    return pl.pallas_call(
-        pack_kernel,
-        out_shape=jax.ShapeDtypeStruct((ranks, 4, piece, W), jnp.float32),
-        in_specs=[anywhere] * 2,
-        out_specs=anywhere,
-        scratch_shapes=[pltpu.SemaphoreType.DMA((4,))],
-        compiler_params=pltpu.CompilerParams(vmem_limit_bytes=ROOM),
-        name="pack_part",
-    )(*(pltpu.with_memory_space_constraint(value, pltpu.HBM) for value in (start, right)))
 
 
 def own_slot(mine, index):
@@ -488,12 +458,20 @@
 
     start = start_core.reshape(ranks, own, piece, width)
     right = right_side.reshape(ranks, own, piece, width)
-    mine = exchange(pack_part(start, right), "rank")
-
-    table = lax.dynamic_slice_in_dim(couplings.reshape(27, height), rank_index * own, own, 1)
+    odd = lax.axis_index("core") == 1
+    packed = jnp.concatenate([start, right], axis=1)
+    mine = exchange(jnp.where(odd, packed[::-1], packed), "rank")
+
+    chunk = jnp.where(odd, ranks - 1 - rank_index, rank_index)
+    table = lax.dynamic_slice_in_dim(couplings.reshape(27, height), chunk * own, own, 1)
     table = jnp.pad(table, ((0, 5), (0, 0))).T[:, :, None]
     table = jnp.broadcast_to(table, (own, 32, width)).reshape(own * 32, width)
-    forward = [(i, i + 1) for i in range(count - 1)]
+    order = [
+        slab * ranks + (part if slab % 2 == 0 else ranks - 1 - part)
+        for slab in range(slabs)
+        for part in range(ranks)
+    ]
+    forward = list(zip(order[:-1], order[1:]))
     backward = [(target, source) for source, target in forward]
 
     ahead, behind, terms = parcel_part(mine, table, left_interface, right_interface)
@@ -515,7 +493,8 @@
 
     rank = jnp.full((1,), rank_index, jnp.int32)
     basis, triangle, interface = final_part(whole.reshape(512, width), alpha, mine, owned, rank)
-    output = exchange(basis, "rank").reshape(height, piece, width)
+    output = exchange(basis, "rank")
+    output = jnp.where(odd, output[::-1], output).reshape(height, piece, width)
     return (output, triangle, interface)
 
 

time: 134 us -> 124 us (0.925)
  Pallas kernels: 22.6 us -> 13.6 us
  blocking collectives: 70 us -> 63.6 us
  waiting for transfers between devices: 18.1 us -> 20.6 us
  other arithmetic: 0.05 us -> 2.45 us
    pallas_call x1 -> x0, Pallas kernels: 9.08 us -> none  [pack_part(): pl.pallas_call(pack_kernel, out_shape=jax.ShapeDtypeStruct((ranks, 4, pie...]
    all_to_all x4, blocking collectives: 70 us -> 63.6 us  [exchange(): return lax.all_to_all(blocks, axis, 0, 0, tiled=True)]
    ppermute x1, starting transfers between devices: 1.92 us -> 5.43 us  [shards(): low = lax.ppermute(ahead, ('x', 'y', 'core', 'rank'), forward)]
    ppermute x1, starting transfers between devices: 4.85 us -> 1.92 us  [shards(): high = lax.ppermute(behind, ('x', 'y', 'core', 'rank'), backward)]
    ppermute x1, waiting for transfers between devices: 1.21 us -> 3.86 us  [shards(): high = lax.ppermute(behind, ('x', 'y', 'core', 'rank'), backward)]
    select_n x0 -> x2, other arithmetic: none -> 1.4 us  [the longest x1 0.74 us: shards(): mine = exchange(jnp.where(odd, packed[::-1], packed), 'rank')]
  transfers between devices with their start and end apart: 4 -> 4, of which waited for: 4 -> 3; matrix products, arithmetic and copies ran while one was open for 0% -> 0% of each run, Pallas kernels for 1% -> 1%
where the time goes in v6:
time: 124 us; the launch traced here: 123 us
  blocking collectives  63.6 us (51%)
  starting transfers between devices  21.7 us (18%)
  waiting for transfers between devices  20.6 us (17%)
  Pallas kernels  13.6 us (11%)
  other arithmetic  2.45 us (2%)
    all_to_all x4, blocking collectives, exchange(): return lax.all_to_all(blocks, axis, 0, 0, tiled=True)  63.6 us
    all_to_all x2, waiting for transfers between devices, exchange(): return lax.all_to_all(blocks, axis, 0, 0, tiled=True)  16.7 us
    all_to_all x2, starting transfers between devices, exchange(): return lax.all_to_all(blocks, axis, 0, 0, tiled=True)  14.4 us
    pallas_call x1, Pallas kernels, final_part(): pl.pallas_call(factor_kernel, out_shape=(pltpu.VMEM((ranks, 2, piece, W),...  5.74 us
    ppermute x1, starting transfers between devices, shards(): low = lax.ppermute(ahead, ('x', 'y', 'core', 'rank'), forward)  5.43 us
    pallas_call x1, Pallas kernels, local_part(): pl.pallas_call(local_kernel, out_shape=(pltpu.VMEM((HALF * 24, W), jnp.fl...  4.82 us
    ppermute x1, waiting for transfers between devices, shards(): high = lax.ppermute(behind, ('x', 'y', 'core', 'rank'), backward)  3.86 us
  transfers between devices with their start and end apart: 4, of which 3 were waited for; matrix products, arithmetic and copies ran while one was open for 0% of the time, Pallas kernels for 1%

profile of v6, /device:TPU:1, one launch (start us, length us, event | category | flops | bytes accessed | tf_op | source)
XLA Modules:
  0.0 123.1 jit_solution(14088697882704638883)
XLA Ops:
  0.6 1.0 pad_maximum_fusion
  1.6 0.7 reverse_select_fusion
  2.4 0.0 copy-start.2
  2.4 0.0 copy-start
  2.4 0.0 copy-start.1
  2.4 11.0 %all-to-all-start = ((f32[8,4,16,128]{3,2,1,0:T(8,128)}), f32[8,4,16,128]{3,2,1,0:T(8,128)S(1)}, u32[]{:S(2)}, u32[]{:S(2)}) async-start(f32[8,4,16,128]{3,2,1,0:T(8,128)} %reverse_select_fusion), calls=%async_computation | async-start | bytes 524288 | tf_op jit(solution)/shard_map/all_to_all | solution.py:17
  13.4 0.0 copy-done.2
  13.4 0.1 constant_dynamic-slice_fusion
  13.5 0.1 copy.14
  13.6 0.1 broadcast_in_dim.21
  13.6 10.2 %all-to-all-done.mine = f32[8,4,16,128]{3,2,1,0:T(8,128)S(1)} async-done(((f32[8,4,16,128]{3,2,1,0:T(8,128)}), f32[8,4,16,128]{3,2,1,0:T(8,128)S(1)}, u32[]{:S(2)}, u32[]{:S(2)}) %all-to-all-start) | async-done | bytes 262176 | tf_op jit(solution)/shard_map/all_to_all | solution.py:17
  23.9 0.1 broadcast_in_dim.22.table
  23.9 0.0 copy-done
  23.9 0.0 copy-done.1
  23.9 1.2 parcel_part.1
  25.1 5.4 %collective-permute-start = (f32[272,128]{1,0:T(8,128)S(1)}, f32[272,128]{1,0:T(8,128)S(1)}, u32[]{:S(2)}, u32[]{:S(2)}) collective-permute-start(f32[272,128]{1,0:T(8,128)S(1)} %get-tuple-element.13.ahead), channel_id=1, source_target_pairs={{0,1},{1,2},{2,3},{3,4},{4,5},{5,6},{6,7},{7,15},{15,14},{14,13},{... | collective-permute-start | bytes 417800 | tf_op jit(solution)/shard_map/ppermute | solution.py:478
  30.5 1.9 %collective-permute-start.1 = (f32[272,128]{1,0:T(8,128)S(1)}, f32[272,128]{1,0:T(8,128)S(1)}, u32[]{:S(2)}, u32[]{:S(2)}) collective-permute-start(f32[272,128]{1,0:T(8,128)S(1)} %get-tuple-element.14.behind), channel_id=1, source_target_pairs={{1,0},{2,1},{3,2},{4,3},{5,4},{6,5},{7,6},{15,7},{14,15},{13,14},{... | collective-permute-start | bytes 417800 | tf_op jit(solution)/shard_map/ppermute | solution.py:479
  32.5 0.6 early_part.1.shifted
  33.0 0.0 collective-permute-done.low
  33.0 3.9 %collective-permute-done.1.high = f32[272,128]{1,0:T(8,128)S(1)} collective-permute-done((f32[272,128]{1,0:T(8,128)S(1)}, f32[272,128]{1,0:T(8,128)S(1)}, u32[]{:S(2)}, u32[]{:S(2)}) %collective-permute-start.1) | collective-permute-done | bytes 139296 | tf_op jit(solution)/shard_map/ppermute | solution.py:479
  36.9 4.8 %local_part.1 = (f32[1536,128]{1,0:T(8,128)S(1)}, f32[256,128]{1,0:T(8,128)S(1)}) custom-call(f32[8,4,16,128]{3,2,1,0:T(8,128)S(1)} %all-to-all-done.mine, f32[272,128]{1,0:T(8,128)S(1)} %collective-permute-done.low, f32[272,128]{1,0:T(8,128)S(1)} %collective-permute-done.1.high, f32[272,128]{1,0:T(8,128)S(1)} %get-tuple-element.13.ahead, ...), custom_call_target="tpu_custom_call" | custom-call | tf_op jit(solution)/shard_map/local_part/pallas_call | solution.py:287
  41.7 17.0 %all_to_all.30 = f32[8,192,128]{2,1,0:T(8,128)S(1)} all-to-all(f32[8,192,128]{2,1,0:T(8,128)S(1)} %bitcast.22), channel_id=1, replica_groups=mesh['x'=4,'y'=8,'core'=2,'rank'=8] {'x','core'}, dimensions={0} | all-to-all | bytes 1572864 | tf_op jit(solution)/shard_map/all_to_all | solution.py:17
  58.8 0.1 copy.16
  58.9 19.5 %all_to_all.31 = f32[64,4,128]{2,1,0:T(4,128)S(1)} all-to-all(f32[64,4,128]{2,1,0:T(4,128)S(1)} %copy.16), channel_id=1, replica_groups=mesh['x'=4,'y'=8,'core'=2,'rank'=8] {'y','rank'}, dimensions={0} | all-to-all | bytes 262144 | tf_op jit(solution)/shard_map/all_to_all | solution.py:17
  78.4 0.1 combine_part.1
  78.5 14.6 %all_to_all.32 = f32[64,1,128]{2,1,0:T(1,128)S(1)} all-to-all(f32[64,1,128]{2,1,0:T(1,128)S(1)} %bitcast.24), channel_id=1, replica_groups=mesh['x'=4,'y'=8,'core'=2,'rank'=8] {'y','rank'}, dimensions={0} | all-to-all | bytes 65536 | tf_op jit(solution)/shard_map/all_to_all | solution.py:17
  93.2 12.4 %all_to_all.33 = f32[8,64,128]{2,1,0:T(8,128)S(1)} all-to-all(f32[8,64,128]{2,1,0:T(8,128)S(1)} %broadcast_in_dim.25), channel_id=1, replica_groups=mesh['x'=4,'y'=8,'core'=2,'rank'=8] {'x','core'}, dimensions={0} | all-to-all | bytes 524288 | tf_op jit(solution)/shard_map/all_to_all | solution.py:17
  105.7 5.7 %factor_part.1 = (f32[8,2,16,128]{3,2,1,0:T(8,128)}, f32[128,128]{1,0:T(8,128)}, f32[128,128]{1,0:T(8,128)S(1)}) custom-call(f32[512,128]{1,0:T(8,128)S(1)} %bitcast.20, f32[8,128]{1,0:T(8,128)S(1)} %get-tuple-element.18.alpha_ref, f32[8,4,16,128]{3,2,1,0:T(8,128)S(1)} %all-to-all-done.mine, f32[256,128]{1,0:T(8,128)S(1)} %get-tuple-element.19.owned), custom_call_target="tpu_custom_call" | custom-call | tf_op jit(solution)/shard_map/factor_part/pallas_call | solution.py:425
  111.4 3.4 %all-to-all-start.5 = ((f32[8,2,16,128]{3,2,1,0:T(8,128)}), f32[8,2,16,128]{3,2,1,0:T(8,128)S(1)}, u32[]{:S(2)}, u32[]{:S(2)}) async-start(f32[8,2,16,128]{3,2,1,0:T(8,128)} %get-tuple-element.20), calls=%async_computation.5 | async-start | bytes 262144 | tf_op jit(solution)/shard_map/all_to_all | solution.py:17
  114.8 1.2 interface_part.1
  115.9 6.5 %all-to-all-done.5 = f32[8,2,16,128]{3,2,1,0:T(8,128)S(1)} async-done(((f32[8,2,16,128]{3,2,1,0:T(8,128)}), f32[8,2,16,128]{3,2,1,0:T(8,128)S(1)}, u32[]{:S(2)}, u32[]{:S(2)}) %all-to-all-start.5) | async-done | bytes 131104 | tf_op jit(solution)/shard_map/all_to_all | solution.py:17
  122.4 0.7 reverse_select_fusion.1
  (7 shorter events, 0.1 us)
Async XLA Ops:
  2.4 11.0 %copy-start.2 = (f32[3,3,3,16]{3,2,1,0:T(4,128)S(1)}, f32[3,3,3,16]{3,2,1,0:T(4,128)}, u32[]{:S(2)}) copy-start(f32[3,3,3,16]{3,2,1,0:T(4,128)} %param.9) | copy-start | bytes 5188
  2.4 21.6 %copy-start = (f32[3,128,128]{2,1,0:T(8,128)S(1)}, f32[3,128,128]{2,1,0:T(8,128)}, u32[]{:S(2)}) copy-start(f32[3,128,128]{2,1,0:T(8,128)} %left_ref.5) | copy-start | bytes 589828
  2.4 21.6 %copy-start.1 = (f32[3,128,128]{2,1,0:T(8,128)S(1)}, f32[3,128,128]{2,1,0:T(8,128)}, u32[]{:S(2)}) copy-start(f32[3,128,128]{2,1,0:T(8,128)} %right_ref.3) | copy-start | bytes 589828
  2.4 21.5 %all-to-all-start = ((f32[8,4,16,128]{3,2,1,0:T(8,128)}), f32[8,4,16,128]{3,2,1,0:T(8,128)S(1)}, u32[]{:S(2)}, u32[]{:S(2)}) async-start(f32[8,4,16,128]{3,2,1,0:T(8,128)} %reverse_select_fusion), calls=%async_computation | async-start | bytes 524288 | tf_op jit(solution)/shard_map/all_to_all | solution.py:17
  25.1 7.9 %collective-permute-start = (f32[272,128]{1,0:T(8,128)S(1)}, f32[272,128]{1,0:T(8,128)S(1)}, u32[]{:S(2)}, u32[]{:S(2)}) collective-permute-start(f32[272,128]{1,0:T(8,128)S(1)} %get-tuple-element.13.ahead), channel_id=1, source_target_pairs={{0,1},{1,2},{2,3},{3,4},{4,5},{5,6},{6,7},{7,15},{15,14},{14,13},{... | collective-permute-start | bytes 417800 | tf_op jit(solution)/shard_map/ppermute | solution.py:478
  30.5 6.4 %collective-permute-start.1 = (f32[272,128]{1,0:T(8,128)S(1)}, f32[272,128]{1,0:T(8,128)S(1)}, u32[]{:S(2)}, u32[]{:S(2)}) collective-permute-start(f32[272,128]{1,0:T(8,128)S(1)} %get-tuple-element.14.behind), channel_id=1, source_target_pairs={{1,0},{2,1},{3,2},{4,3},{5,4},{6,5},{7,6},{15,7},{14,15},{13,14},{... | collective-permute-start | bytes 417800 | tf_op jit(solution)/shard_map/ppermute | solution.py:479
  111.4 11.0 %all-to-all-start.5 = ((f32[8,2,16,128]{3,2,1,0:T(8,128)}), f32[8,2,16,128]{3,2,1,0:T(8,128)S(1)}, u32[]{:S(2)}, u32[]{:S(2)}) async-start(f32[8,2,16,128]{3,2,1,0:T(8,128)} %get-tuple-element.20), calls=%async_computation.5 | async-start | bytes 262144 | tf_op jit(solution)/shard_map/all_to_all | solution.py:17

commit v7 on v6

--- a/solution.py
+++ b/solution.py
@@ -51,6 +51,10 @@
 
 def near(*values):
     return [pltpu.with_memory_space_constraint(value, pltpu.VMEM) for value in values]
+
+
+def part_of(whole, part):
+    return jnp.concatenate([whole[64 * y + 8 * part : 64 * y + 8 * part + 8] for y in range(8)])
 
 
 def own_slot(mine, index):
@@ -166,10 +170,12 @@
     )(*near(mine, table, left_interface, right_interface))
 
 
-def early_kernel(mine, table, left_ref, shifted, mixed):
+def early_kernel(mine, table, left_ref, shifted, square, mixed):
     left_rows = halves(left_ref[...].reshape(3 * W, W))
     stack = halves(jnp.concatenate([own_slot(mine, 0), own_slot(mine, 1)], axis=0))
     mixed[...] = split_product(stack, left_rows, 1).reshape(2, W, 3 * W)
+    wide = jnp.concatenate([own_slot(mine, 0), own_slot(mine, 1)], axis=1)
+    square[...] = product_t(wide, wide)
     for i in range(2):
         present = [(1 - i + k, mixed_rows(mixed, k)) for k in range(2)]
         couple(own_row(table, i), present, moved_of(shifted, (), i)[1], None, True)
@@ -179,9 +185,12 @@
     vmem = pl.BlockSpec(memory_space=pltpu.VMEM)
     return pl.pallas_call(
         early_kernel,
-        out_shape=pltpu.VMEM((3 * W, 2 * W), jnp.float32),
+        out_shape=(
+            pltpu.VMEM((3 * W, 2 * W), jnp.float32),
+            pltpu.VMEM((W, W), jnp.float32),
+        ),
         in_specs=[vmem] * 3,
-        out_specs=vmem,
+        out_specs=(vmem, vmem),
         scratch_shapes=[pltpu.VMEM((2, W, 3 * W), jnp.float32)],
         compiler_params=pltpu.CompilerParams(vmem_limit_bytes=ROOM),
         name="early_part",
@@ -197,6 +206,7 @@
     own_terms,
     table,
     shifted,
+    start_gram,
     left_ref,
     right_ref,
     blocks,
@@ -263,26 +273,29 @@
     split = halves(both)
     forms = [split_product(halves(moved[u]), split, 1) for u in range(2)]
     tables = [forms[0][:, :W], forms[0][:, W:] + forms[1][:, :W], forms[1][:, W:]]
-    square = product_t(both, both)
-    grams = [square[:W, :W], square[:W, W:] + square[W:, :W], square[W:, W:]]
+    square = product_t(both, both[W:])
+    grams = [start_gram[...], square[:W] + square[:W].T, square[W:]]
     row, lane = iotas((HALF, W))
+
+    def put(index, value):
+        for y in range(8):
+            blocks[pl.ds(24 * y + index, 8, stride=192), :] = value[8 * y : 8 * y + 8]
+
     for version in range(3):
         gram = grams[version]
         upper, under = gram[:HALF], gram[HALF:]
         for part in range(6):
-            blocks[pl.ds(8 * version + part, HALF, stride=24), :] = tables[version][
-                part * HALF : (part + 1) * HALF
-            ]
+            put(8 * version + part, tables[version][part * HALF : (part + 1) * HALF])
         fold = jnp.where(lane <= row + HALF, under, pltpu.roll(upper, HALF, 1))
-        blocks[pl.ds(8 * version + 6, HALF, stride=24), :] = fold
+        put(8 * version + 6, fold)
         diagonal = jnp.sum(jnp.where(lane == row, upper, 0.0), axis=1, keepdims=True)
         extra = jnp.where(lane == 0, diagonal, 0.0)
         if version == 0:
             extra = jnp.where(lane == 1, along, jnp.where(lane == 2, energy, extra))
-        blocks[pl.ds(8 * version + 7, HALF, stride=24), :] = extra
-
-
-def local_part(mine, low, high, ahead, behind, terms, table, shifted, left_interface, right_interface):
+        put(8 * version + 7, extra)
+
+
+def local_part(mine, low, high, ahead, behind, terms, table, early, left_interface, right_interface):
     vmem = pl.BlockSpec(memory_space=pltpu.VMEM)
     return pl.pallas_call(
         local_kernel,
@@ -290,7 +303,7 @@
             pltpu.VMEM((HALF * 24, W), jnp.float32),
             pltpu.VMEM((2 * W, W), jnp.float32),
         ),
-        in_specs=[vmem] * 10,
+        in_specs=[vmem] * 11,
         out_specs=(vmem, vmem),
         scratch_shapes=[
             pltpu.VMEM((4, 3 * W, W), jnp.float32),
@@ -310,7 +323,7 @@
             behind,
             terms,
             table,
-            shifted,
+            *early,
             left_interface,
             right_interface,
         )
@@ -338,7 +351,7 @@
     return pl.pallas_call(
         kernel,
         out_shape=(
-            pltpu.VMEM((got.shape[0] // 4, W), jnp.float32),
+            pltpu.VMEM((8, W), jnp.float32),
             pltpu.VMEM((8, W), jnp.float32),
         ),
         in_specs=[vmem],
@@ -350,8 +363,8 @@
 
 def factor_kernel(whole, alpha_ref, mine, owned, basis, triangle, inverse, table):
     row, lane = iotas((HALF, W))
-    fold = whole[pl.ds(6, HALF, stride=8), :]
-    extra = whole[pl.ds(7, HALF, stride=8), :]
+    fold = part_of(whole, 6)
+    extra = part_of(whole, 7)
     under = jnp.where(lane <= row + HALF, fold, 0.0)
     upper = jnp.where((lane > row) & (lane < HALF), pltpu.roll(fold, HALF, 1), 0.0)
     upper = upper + jnp.where(lane == row, jnp.broadcast_to(extra[:, :1], (HALF, W)), 0.0)
@@ -413,8 +426,8 @@
     mine = inverse[pl.ds(start, rows), :]
     parts = []
     for beta in range(3):
-        halves = [whole[pl.ds(2 * beta + h, HALF, stride=8), :] for h in range(2)]
-        parts.append(product(mine, jnp.concatenate(halves, axis=0)))
+        both = jnp.concatenate([part_of(whole, 2 * beta + h) for h in range(2)])
+        parts.append(product(mine, both))
     result = product_t(jnp.concatenate(parts, axis=0), inverse[...])
     out[...] = result.reshape(3, rows, W)
 
@@ -477,9 +490,9 @@
     ahead, behind, terms = parcel_part(mine, table, left_interface, right_interface)
     low = lax.ppermute(ahead, ("x", "y", "core", "rank"), forward)
     high = lax.ppermute(behind, ("x", "y", "core", "rank"), backward)
-    shifted = early_part(mine, table, left_interface)
+    early = early_part(mine, table, left_interface)
     blocks, owned = local_part(
-        mine, low, high, ahead, behind, terms, table, shifted, left_interface, right_interface
+        mine, low, high, ahead, behind, terms, table, early, left_interface, right_interface
     )
 
     block = jnp.sum(exchange(blocks.reshape(8, 192, width), ("x", "core")), axis=0)
@@ -488,8 +501,8 @@
     block = jnp.concatenate([block.transpose(0, 2, 1, 3), sums], axis=2)
     block = exchange(block.reshape(64, 4, width), ("y", "rank")).reshape(256, width)
     block, alpha = combine_part(block, scale)
-    block = exchange(block.reshape(64, 1, width), ("y", "rank")).reshape(64, width)
-    whole = exchange(jnp.broadcast_to(block, (8, 64, width)), ("x", "core"))
+    block = exchange(block.reshape(8, 1, width), ("x", "core")).reshape(8, width)
+    whole = exchange(jnp.broadcast_to(block, (64, 8, width)), ("y", "rank"))
 
     rank = jnp.full((1,), rank_index, jnp.int32)
     basis, triangle, interface = final_part(whole.reshape(512, width), alpha, mine, owned, rank)

time: 124 us -> 125 us (level)
  no operation moved by 1% of the time
where the time goes in v7:
time: 125 us; the launch traced here: 123 us
  blocking collectives  62.7 us (50%)
  starting transfers between devices  22 us (18%)
  waiting for transfers between devices  20.8 us (17%)
  Pallas kernels  13.9 us (11%)
  other arithmetic  2.44 us (2%)
    all_to_all x4, blocking collectives, exchange(): return lax.all_to_all(blocks, axis, 0, 0, tiled=True)  62.7 us
    all_to_all x2, waiting for transfers between devices, exchange(): return lax.all_to_all(blocks, axis, 0, 0, tiled=True)  17 us
    all_to_all x2, starting transfers between devices, exchange(): return lax.all_to_all(blocks, axis, 0, 0, tiled=True)  14.6 us
    pallas_call x1, Pallas kernels, final_part(): pl.pallas_call(factor_kernel, out_shape=(pltpu.VMEM((ranks, 2, piece, W),...  5.73 us
    ppermute x1, starting transfers between devices, shards(): low = lax.ppermute(ahead, ('x', 'y', 'core', 'rank'), forward)  5.43 us
    pallas_call x1, Pallas kernels, local_part(): pl.pallas_call(local_kernel, out_shape=(pltpu.VMEM((HALF * 24, W), jnp.fl...  5.1 us
    ppermute x1, waiting for transfers between devices, shards(): high = lax.ppermute(behind, ('x', 'y', 'core', 'rank'), backward)  3.77 us
  transfers between devices with their start and end apart: 4, of which 3 were waited for; matrix products, arithmetic and copies ran while one was open for 0% of the time, Pallas kernels for 1%

profile of v7, /device:TPU:1, one launch (start us, length us, event | category | flops | bytes accessed | tf_op | source)
XLA Modules:
  0.0 123.0 jit_solution(8379444133520383831)
XLA Ops:
  0.6 1.0 pad_maximum_fusion
  1.6 0.7 reverse_select_fusion
  2.4 0.0 copy-start.2
  2.4 0.0 copy-start
  2.4 0.0 copy-start.1
  2.4 11.0 %all-to-all-start = ((f32[8,4,16,128]{3,2,1,0:T(8,128)}), f32[8,4,16,128]{3,2,1,0:T(8,128)S(1)}, u32[]{:S(2)}, u32[]{:S(2)}) async-start(f32[8,4,16,128]{3,2,1,0:T(8,128)} %reverse_select_fusion), calls=%async_computation | async-start | bytes 524288 | tf_op jit(solution)/shard_map/all_to_all | solution.py:17
  13.4 0.0 copy-done.2
  13.4 0.1 constant_dynamic-slice_fusion
  13.5 0.1 copy.14
  13.5 0.1 broadcast_in_dim.21
  13.6 10.2 %all-to-all-done.mine = f32[8,4,16,128]{3,2,1,0:T(8,128)S(1)} async-done(((f32[8,4,16,128]{3,2,1,0:T(8,128)}), f32[8,4,16,128]{3,2,1,0:T(8,128)S(1)}, u32[]{:S(2)}, u32[]{:S(2)}) %all-to-all-start) | async-done | bytes 262176 | tf_op jit(solution)/shard_map/all_to_all | solution.py:17
  23.9 0.1 broadcast_in_dim.22.table
  23.9 0.0 copy-done
  23.9 0.0 copy-done.1
  23.9 1.2 parcel_part.1
  25.1 5.4 %collective-permute-start = (f32[272,128]{1,0:T(8,128)S(1)}, f32[272,128]{1,0:T(8,128)S(1)}, u32[]{:S(2)}, u32[]{:S(2)}) collective-permute-start(f32[272,128]{1,0:T(8,128)S(1)} %get-tuple-element.15.ahead), channel_id=1, source_target_pairs={{0,1},{1,2},{2,3},{3,4},{4,5},{5,6},{6,7},{7,15},{15,14},{14,13},{... | collective-permute-start | bytes 417800 | tf_op jit(solution)/shard_map/ppermute | solution.py:491
  30.5 1.9 %collective-permute-start.1 = (f32[272,128]{1,0:T(8,128)S(1)}, f32[272,128]{1,0:T(8,128)S(1)}, u32[]{:S(2)}, u32[]{:S(2)}) collective-permute-start(f32[272,128]{1,0:T(8,128)S(1)} %get-tuple-element.16.behind), channel_id=1, source_target_pairs={{1,0},{2,1},{3,2},{4,3},{5,4},{6,5},{7,6},{15,7},{14,15},{13,14},{... | collective-permute-start | bytes 417800 | tf_op jit(solution)/shard_map/ppermute | solution.py:492
  32.5 0.7 early_part.1
  33.1 0.0 collective-permute-done.low
  33.1 3.8 %collective-permute-done.1.high = f32[272,128]{1,0:T(8,128)S(1)} collective-permute-done((f32[272,128]{1,0:T(8,128)S(1)}, f32[272,128]{1,0:T(8,128)S(1)}, u32[]{:S(2)}, u32[]{:S(2)}) %collective-permute-start.1) | collective-permute-done | bytes 139296 | tf_op jit(solution)/shard_map/ppermute | solution.py:492
  36.9 5.1 %local_part.1 = (f32[1536,128]{1,0:T(8,128)S(1)}, f32[256,128]{1,0:T(8,128)S(1)}) custom-call(f32[8,4,16,128]{3,2,1,0:T(8,128)S(1)} %all-to-all-done.mine, f32[272,128]{1,0:T(8,128)S(1)} %collective-permute-done.low, f32[272,128]{1,0:T(8,128)S(1)} %collective-permute-done.1.high, f32[272,128]{1,0:T(8,128)S(1)} %get-tuple-element.15.ahead, ...), custom_call_target="tpu_custom_call" | custom-call | tf_op jit(solution)/shard_map/local_part/pallas_call | solution.py:300
  42.0 17.0 %all_to_all.30 = f32[8,192,128]{2,1,0:T(8,128)S(1)} all-to-all(f32[8,192,128]{2,1,0:T(8,128)S(1)} %bitcast.22), channel_id=1, replica_groups=mesh['x'=4,'y'=8,'core'=2,'rank'=8] {'x','core'}, dimensions={0} | all-to-all | bytes 1572864 | tf_op jit(solution)/shard_map/all_to_all | solution.py:17
  59.1 0.1 copy.16
  59.2 19.5 %all_to_all.31 = f32[64,4,128]{2,1,0:T(4,128)S(1)} all-to-all(f32[64,4,128]{2,1,0:T(4,128)S(1)} %copy.16), channel_id=1, replica_groups=mesh['x'=4,'y'=8,'core'=2,'rank'=8] {'y','rank'}, dimensions={0} | all-to-all | bytes 262144 | tf_op jit(solution)/shard_map/all_to_all | solution.py:17
  78.7 0.1 combine_part.1
  78.8 9.4 %all_to_all.32 = f32[8,1,128]{2,1,0:T(1,128)S(1)} all-to-all(f32[8,1,128]{2,1,0:T(1,128)S(1)} %bitcast.24), channel_id=1, replica_groups=mesh['x'=4,'y'=8,'core'=2,'rank'=8] {'x','core'}, dimensions={0} | all-to-all | bytes 8192 | tf_op jit(solution)/shard_map/all_to_all | solution.py:17
  88.2 16.8 %all_to_all.33 = f32[64,8,128]{2,1,0:T(8,128)S(1)} all-to-all(f32[64,8,128]{2,1,0:T(8,128)S(1)} %broadcast_in_dim.25), channel_id=1, replica_groups=mesh['x'=4,'y'=8,'core'=2,'rank'=8] {'y','rank'}, dimensions={0} | all-to-all | bytes 524288 | tf_op jit(solution)/shard_map/all_to_all | solution.py:17
  105.0 5.7 %factor_part.1 = (f32[8,2,16,128]{3,2,1,0:T(8,128)}, f32[128,128]{1,0:T(8,128)}, f32[128,128]{1,0:T(8,128)S(1)}) custom-call(f32[512,128]{1,0:T(8,128)S(1)} %bitcast.20, f32[8,128]{1,0:T(8,128)S(1)} %get-tuple-element.22.alpha_ref, f32[8,4,16,128]{3,2,1,0:T(8,128)S(1)} %all-to-all-done.mine, f32[256,128]{1,0:T(8,128)S(1)} %get-tuple-element.23.owned), custom_call_target="tpu_custom_call" | custom-call | tf_op jit(solution)/shard_map/factor_part/pallas_call | solution.py:438
  110.7 3.7 %all-to-all-start.5 = ((f32[8,2,16,128]{3,2,1,0:T(8,128)}), f32[8,2,16,128]{3,2,1,0:T(8,128)S(1)}, u32[]{:S(2)}, u32[]{:S(2)}) async-start(f32[8,2,16,128]{3,2,1,0:T(8,128)} %get-tuple-element.24), calls=%async_computation.5 | async-start | bytes 262144 | tf_op jit(solution)/shard_map/all_to_all | solution.py:17
  114.4 1.2 interface_part.1
  115.6 6.8 %all-to-all-done.5 = f32[8,2,16,128]{3,2,1,0:T(8,128)S(1)} async-done(((f32[8,2,16,128]{3,2,1,0:T(8,128)}), f32[8,2,16,128]{3,2,1,0:T(8,128)S(1)}, u32[]{:S(2)}, u32[]{:S(2)}) %all-to-all-start.5) | async-done | bytes 131104 | tf_op jit(solution)/shard_map/all_to_all | solution.py:17
  122.3 0.7 reverse_select_fusion.1
  (7 shorter events, 0.1 us)
Async XLA Ops:
  2.4 11.0 %copy-start.2 = (f32[3,3,3,16]{3,2,1,0:T(4,128)S(1)}, f32[3,3,3,16]{3,2,1,0:T(4,128)}, u32[]{:S(2)}) copy-start(f32[3,3,3,16]{3,2,1,0:T(4,128)} %param.9) | copy-start | bytes 5188
  2.4 21.6 %copy-start = (f32[3,128,128]{2,1,0:T(8,128)S(1)}, f32[3,128,128]{2,1,0:T(8,128)}, u32[]{:S(2)}) copy-start(f32[3,128,128]{2,1,0:T(8,128)} %left_ref.5) | copy-start | bytes 589828
  2.4 21.6 %copy-start.1 = (f32[3,128,128]{2,1,0:T(8,128)S(1)}, f32[3,128,128]{2,1,0:T(8,128)}, u32[]{:S(2)}) copy-start(f32[3,128,128]{2,1,0:T(8,128)} %right_ref.3) | copy-start | bytes 589828
  2.4 21.5 %all-to-all-start = ((f32[8,4,16,128]{3,2,1,0:T(8,128)}), f32[8,4,16,128]{3,2,1,0:T(8,128)S(1)}, u32[]{:S(2)}, u32[]{:S(2)}) async-start(f32[8,4,16,128]{3,2,1,0:T(8,128)} %reverse_select_fusion), calls=%async_computation | async-start | bytes 524288 | tf_op jit(solution)/shard_map/all_to_all | solution.py:17
  25.1 8.0 %collective-permute-start = (f32[272,128]{1,0:T(8,128)S(1)}, f32[272,128]{1,0:T(8,128)S(1)}, u32[]{:S(2)}, u32[]{:S(2)}) collective-permute-start(f32[272,128]{1,0:T(8,128)S(1)} %get-tuple-element.15.ahead), channel_id=1, source_target_pairs={{0,1},{1,2},{2,3},{3,4},{4,5},{5,6},{6,7},{7,15},{15,14},{14,13},{... | collective-permute-start | bytes 417800 | tf_op jit(solution)/shard_map/ppermute | solution.py:491
  30.5 6.4 %collective-permute-start.1 = (f32[272,128]{1,0:T(8,128)S(1)}, f32[272,128]{1,0:T(8,128)S(1)}, u32[]{:S(2)}, u32[]{:S(2)}) collective-permute-start(f32[272,128]{1,0:T(8,128)S(1)} %get-tuple-element.16.behind), channel_id=1, source_target_pairs={{1,0},{2,1},{3,2},{4,3},{5,4},{6,5},{7,6},{15,7},{14,15},{13,14},{... | collective-permute-start | bytes 417800 | tf_op jit(solution)/shard_map/ppermute | solution.py:492
  110.7 11.6 %all-to-all-start.5 = ((f32[8,2,16,128]{3,2,1,0:T(8,128)}), f32[8,2,16,128]{3,2,1,0:T(8,128)S(1)}, u32[]{:S(2)}, u32[]{:S(2)}) async-start(f32[8,2,16,128]{3,2,1,0:T(8,128)} %get-tuple-element.24), calls=%async_computation.5 | async-start | bytes 262144 | tf_op jit(solution)/shard_map/all_to_all | solution.py:17

commit v8 on v6

--- a/solution.py
+++ b/solution.py
@@ -9,7 +9,7 @@
 highest = lax.Precision.HIGHEST
 W = 128
 HALF = W // 2
-SIZE = 16
+SIZE = 8
 ROOM = 16 * 2**20
 
 

time: 124 us -> 126 us (1.016)
  Pallas kernels: 13.6 us -> 16 us
    pallas_call x1, Pallas kernels: 5.74 us -> 8.15 us  [final_part(): pl.pallas_call(factor_kernel, out_shape=(pltpu.VMEM((ranks, 2, piece, W),...]
where the time goes in v8:
time: 126 us
  blocking collectives  63.6 us (50%)
  starting transfers between devices  21.7 us (17%)
  waiting for transfers between devices  20.6 us (16%)
  Pallas kernels  16 us (13%)
  other arithmetic  2.45 us (2%)
    all_to_all x4, blocking collectives, exchange(): return lax.all_to_all(blocks, axis, 0, 0, tiled=True)  63.6 us
    all_to_all x2, waiting for transfers between devices, exchange(): return lax.all_to_all(blocks, axis, 0, 0, tiled=True)  16.7 us
    all_to_all x2, starting transfers between devices, exchange(): return lax.all_to_all(blocks, axis, 0, 0, tiled=True)  14.4 us
    pallas_call x1, Pallas kernels, final_part(): pl.pallas_call(factor_kernel, out_shape=(pltpu.VMEM((ranks, 2, piece, W),...  8.15 us
    ppermute x1, starting transfers between devices, shards(): low = lax.ppermute(ahead, ('x', 'y', 'core', 'rank'), forward)  5.43 us
    pallas_call x1, Pallas kernels, local_part(): pl.pallas_call(local_kernel, out_shape=(pltpu.VMEM((HALF * 24, W), jnp.fl...  4.82 us
    ppermute x1, waiting for transfers between devices, shards(): high = lax.ppermute(behind, ('x', 'y', 'core', 'rank'), backward)  3.86 us
  transfers between devices with their start and end apart: 4, of which 3 were waited for; matrix products, arithmetic and copies ran while one was open for 0% of the time, Pallas kernels for 1%

profile of v8, /device:TPU:1, one launch (start us, length us, event | category | flops | bytes accessed | tf_op | source)
XLA Modules:
  0.0 125.5 jit_solution(8946326183255586710)
XLA Ops:
  0.6 1.0 pad_maximum_fusion
  1.6 0.7 reverse_select_fusion
  2.4 0.0 copy-start.2
  2.4 0.0 copy-start
  2.4 0.0 copy-start.1
  2.4 11.0 %all-to-all-start = ((f32[8,4,16,128]{3,2,1,0:T(8,128)}), f32[8,4,16,128]{3,2,1,0:T(8,128)S(1)}, u32[]{:S(2)}, u32[]{:S(2)}) async-start(f32[8,4,16,128]{3,2,1,0:T(8,128)} %reverse_select_fusion), calls=%async_computation | async-start | bytes 524288 | tf_op jit(solution)/shard_map/all_to_all | solution.py:17
  13.4 0.0 copy-done.2
  13.4 0.1 constant_dynamic-slice_fusion
  13.5 0.1 copy.14
  13.6 0.1 broadcast_in_dim.21
  13.6 10.2 %all-to-all-done.mine = f32[8,4,16,128]{3,2,1,0:T(8,128)S(1)} async-done(((f32[8,4,16,128]{3,2,1,0:T(8,128)}), f32[8,4,16,128]{3,2,1,0:T(8,128)S(1)}, u32[]{:S(2)}, u32[]{:S(2)}) %all-to-all-start) | async-done | bytes 262176 | tf_op jit(solution)/shard_map/all_to_all | solution.py:17
  23.9 0.1 broadcast_in_dim.22.table
  23.9 0.0 copy-done
  23.9 0.0 copy-done.1
  23.9 1.2 parcel_part.1
  25.1 5.4 %collective-permute-start = (f32[272,128]{1,0:T(8,128)S(1)}, f32[272,128]{1,0:T(8,128)S(1)}, u32[]{:S(2)}, u32[]{:S(2)}) collective-permute-start(f32[272,128]{1,0:T(8,128)S(1)} %get-tuple-element.13.ahead), channel_id=1, source_target_pairs={{0,1},{1,2},{2,3},{3,4},{4,5},{5,6},{6,7},{7,15},{15,14},{14,13},{... | collective-permute-start | bytes 417800 | tf_op jit(solution)/shard_map/ppermute | solution.py:478
  30.5 1.9 %collective-permute-start.1 = (f32[272,128]{1,0:T(8,128)S(1)}, f32[272,128]{1,0:T(8,128)S(1)}, u32[]{:S(2)}, u32[]{:S(2)}) collective-permute-start(f32[272,128]{1,0:T(8,128)S(1)} %get-tuple-element.14.behind), channel_id=1, source_target_pairs={{1,0},{2,1},{3,2},{4,3},{5,4},{6,5},{7,6},{15,7},{14,15},{13,14},{... | collective-permute-start | bytes 417800 | tf_op jit(solution)/shard_map/ppermute | solution.py:479
  32.5 0.6 early_part.1.shifted
  33.0 0.0 collective-permute-done.low
  33.0 3.9 %collective-permute-done.1.high = f32[272,128]{1,0:T(8,128)S(1)} collective-permute-done((f32[272,128]{1,0:T(8,128)S(1)}, f32[272,128]{1,0:T(8,128)S(1)}, u32[]{:S(2)}, u32[]{:S(2)}) %collective-permute-start.1) | collective-permute-done | bytes 139296 | tf_op jit(solution)/shard_map/ppermute | solution.py:479
  36.9 4.8 %local_part.1 = (f32[1536,128]{1,0:T(8,128)S(1)}, f32[256,128]{1,0:T(8,128)S(1)}) custom-call(f32[8,4,16,128]{3,2,1,0:T(8,128)S(1)} %all-to-all-done.mine, f32[272,128]{1,0:T(8,128)S(1)} %collective-permute-done.low, f32[272,128]{1,0:T(8,128)S(1)} %collective-permute-done.1.high, f32[272,128]{1,0:T(8,128)S(1)} %get-tuple-element.13.ahead, ...), custom_call_target="tpu_custom_call" | custom-call | tf_op jit(solution)/shard_map/local_part/pallas_call | solution.py:287
  41.7 17.0 %all_to_all.30 = f32[8,192,128]{2,1,0:T(8,128)S(1)} all-to-all(f32[8,192,128]{2,1,0:T(8,128)S(1)} %bitcast.22), channel_id=1, replica_groups=mesh['x'=4,'y'=8,'core'=2,'rank'=8] {'x','core'}, dimensions={0} | all-to-all | bytes 1572864 | tf_op jit(solution)/shard_map/all_to_all | solution.py:17
  58.8 0.1 copy.16
  58.9 19.5 %all_to_all.31 = f32[64,4,128]{2,1,0:T(4,128)S(1)} all-to-all(f32[64,4,128]{2,1,0:T(4,128)S(1)} %copy.16), channel_id=1, replica_groups=mesh['x'=4,'y'=8,'core'=2,'rank'=8] {'y','rank'}, dimensions={0} | all-to-all | bytes 262144 | tf_op jit(solution)/shard_map/all_to_all | solution.py:17
  78.4 0.1 combine_part.1
  78.5 14.6 %all_to_all.32 = f32[64,1,128]{2,1,0:T(1,128)S(1)} all-to-all(f32[64,1,128]{2,1,0:T(1,128)S(1)} %bitcast.24), channel_id=1, replica_groups=mesh['x'=4,'y'=8,'core'=2,'rank'=8] {'y','rank'}, dimensions={0} | all-to-all | bytes 65536 | tf_op jit(solution)/shard_map/all_to_all | solution.py:17
  93.2 12.4 %all_to_all.33 = f32[8,64,128]{2,1,0:T(8,128)S(1)} all-to-all(f32[8,64,128]{2,1,0:T(8,128)S(1)} %broadcast_in_dim.25), channel_id=1, replica_groups=mesh['x'=4,'y'=8,'core'=2,'rank'=8] {'x','core'}, dimensions={0} | all-to-all | bytes 524288 | tf_op jit(solution)/shard_map/all_to_all | solution.py:17
  105.7 8.1 %factor_part.1 = (f32[8,2,16,128]{3,2,1,0:T(8,128)}, f32[128,128]{1,0:T(8,128)}, f32[128,128]{1,0:T(8,128)S(1)}) custom-call(f32[512,128]{1,0:T(8,128)S(1)} %bitcast.20, f32[8,128]{1,0:T(8,128)S(1)} %get-tuple-element.18.alpha_ref, f32[8,4,16,128]{3,2,1,0:T(8,128)S(1)} %all-to-all-done.mine, f32[256,128]{1,0:T(8,128)S(1)} %get-tuple-element.19.owned), custom_call_target="tpu_custom_call" | custom-call | tf_op jit(solution)/shard_map/factor_part/pallas_call | solution.py:425
  113.8 3.4 %all-to-all-start.5 = ((f32[8,2,16,128]{3,2,1,0:T(8,128)}), f32[8,2,16,128]{3,2,1,0:T(8,128)S(1)}, u32[]{:S(2)}, u32[]{:S(2)}) async-start(f32[8,2,16,128]{3,2,1,0:T(8,128)} %get-tuple-element.20), calls=%async_computation.5 | async-start | bytes 262144 | tf_op jit(solution)/shard_map/all_to_all | solution.py:17
  117.2 1.2 interface_part.1
  118.4 6.5 %all-to-all-done.5 = f32[8,2,16,128]{3,2,1,0:T(8,128)S(1)} async-done(((f32[8,2,16,128]{3,2,1,0:T(8,128)}), f32[8,2,16,128]{3,2,1,0:T(8,128)S(1)}, u32[]{:S(2)}, u32[]{:S(2)}) %all-to-all-start.5) | async-done | bytes 131104 | tf_op jit(solution)/shard_map/all_to_all | solution.py:17
  124.8 0.7 reverse_select_fusion.1
  (7 shorter events, 0.1 us)
Async XLA Ops:
  2.4 11.0 %copy-start.2 = (f32[3,3,3,16]{3,2,1,0:T(4,128)S(1)}, f32[3,3,3,16]{3,2,1,0:T(4,128)}, u32[]{:S(2)}) copy-start(f32[3,3,3,16]{3,2,1,0:T(4,128)} %param.9) | copy-start | bytes 5188
  2.4 21.6 %copy-start = (f32[3,128,128]{2,1,0:T(8,128)S(1)}, f32[3,128,128]{2,1,0:T(8,128)}, u32[]{:S(2)}) copy-start(f32[3,128,128]{2,1,0:T(8,128)} %left_ref.5) | copy-start | bytes 589828
  2.4 21.6 %copy-start.1 = (f32[3,128,128]{2,1,0:T(8,128)S(1)}, f32[3,128,128]{2,1,0:T(8,128)}, u32[]{:S(2)}) copy-start(f32[3,128,128]{2,1,0:T(8,128)} %right_ref.3) | copy-start | bytes 589828
  2.4 21.5 %all-to-all-start = ((f32[8,4,16,128]{3,2,1,0:T(8,128)}), f32[8,4,16,128]{3,2,1,0:T(8,128)S(1)}, u32[]{:S(2)}, u32[]{:S(2)}) async-start(f32[8,4,16,128]{3,2,1,0:T(8,128)} %reverse_select_fusion), calls=%async_computation | async-start | bytes 524288 | tf_op jit(solution)/shard_map/all_to_all | solution.py:17
  25.1 7.9 %collective-permute-start = (f32[272,128]{1,0:T(8,128)S(1)}, f32[272,128]{1,0:T(8,128)S(1)}, u32[]{:S(2)}, u32[]{:S(2)}) collective-permute-start(f32[272,128]{1,0:T(8,128)S(1)} %get-tuple-element.13.ahead), channel_id=1, source_target_pairs={{0,1},{1,2},{2,3},{3,4},{4,5},{5,6},{6,7},{7,15},{15,14},{14,13},{... | collective-permute-start | bytes 417800 | tf_op jit(solution)/shard_map/ppermute | solution.py:478
  30.5 6.4 %collective-permute-start.1 = (f32[272,128]{1,0:T(8,128)S(1)}, f32[272,128]{1,0:T(8,128)S(1)}, u32[]{:S(2)}, u32[]{:S(2)}) collective-permute-start(f32[272,128]{1,0:T(8,128)S(1)} %get-tuple-element.14.behind), channel_id=1, source_target_pairs={{1,0},{2,1},{3,2},{4,3},{5,4},{6,5},{7,6},{15,7},{14,15},{13,14},{... | collective-permute-start | bytes 417800 | tf_op jit(solution)/shard_map/ppermute | solution.py:479
  113.8 11.0 %all-to-all-start.5 = ((f32[8,2,16,128]{3,2,1,0:T(8,128)}), f32[8,2,16,128]{3,2,1,0:T(8,128)S(1)}, u32[]{:S(2)}, u32[]{:S(2)}) async-start(f32[8,2,16,128]{3,2,1,0:T(8,128)} %get-tuple-element.20), calls=%async_computation.5 | async-start | bytes 262144 | tf_op jit(solution)/shard_map/all_to_all | solution.py:17
